TPU v7x, 128 devices: a whole 4x4x4 slice. The times are simulated.
128 devices in a mesh: px: 8 (over x, core), py: 16 (over y, z).
Axes of the slice: x: 4, y: 4, z: 4, core: 2. Of those that a mesh axis runs over, the one named last changes fastest.
Arguments:
- cell_ids: int32 [131072, 128], P(('px', 'py')), may hold values from 0 to 32767
- masses: bfloat16 [131072, 128], P(('px', 'py')), may hold values from 0.5 to 2
- block_dest: int32 [131072, 1], P(('px', 'py')), may hold values from 0 to 1023; in each aligned block of 1024 rows (0 to 1023, 1024 to 2047, ...) at most 2 rows name the same one
- block_count: int32 [131072], P(('px', 'py')), may hold values from 1 to 128
- screen: float32 [8], replicated, may hold values from 0.02 to 0.2
Outputs:
- potential_modes: float32 [8, 128, 256], P(None, None, ('px', 'py'))
Inputs may be any that keep to these rules, and one draw needn't show every extreme that they name: `block_dest`: tile t lies on device t // 8 (devices numbered px-major) and plane t % 8. Among the 1024 blocks of one device no tile is named more than 2 times, a bound that some block reaches. `block_count`: the live particles of a block are its first ones. `cell_ids`: A cell c is row c // 128 and column c % (128) of the tile.
All inputs are finite; a program needn't handle non-finite values.
Results may differ from a plain program's by a relative error of at most 0.0003.
Values may be sent and summed in bfloat16 or wider, within the bound.
A program may use at most 64 MiB of HBM per device.

v0:
```python
import math

import jax
import jax.numpy as jnp
from jax import lax
from jax.sharding import PartitionSpec as P

NY = 2048
NZ = 2048
KY = 128
KZ = 128
CAP = 2


HIGHEST_PREC = lax.Precision.HIGHEST


def column_table(col_count):
    col_index = lax.broadcasted_iota(jnp.int32, (col_count, 2 * KZ), 0)
    col_slot = lax.broadcasted_iota(jnp.int32, (col_count, 2 * KZ), 1)
    col_freq = col_slot // 2 - KZ // 2
    col_phase = 2.0 * math.pi / NZ * jnp.remainder(col_freq * col_index, NZ).astype(jnp.float32)
    return jnp.where(col_slot % 2 == 0, jnp.cos(col_phase), -jnp.sin(col_phase))


def row_transform(row_coord, columns):
    y_freq = lax.broadcasted_iota(jnp.int32, row_coord.shape, 0) - KY // 2
    yphase = 2.0 * math.pi / NY * jnp.remainder(y_freq * row_coord, NY).astype(jnp.float32)
    cos_part = jnp.einsum("kp,lpc->lkc", jnp.cos(yphase), columns, precision=HIGHEST_PREC)
    sin_part = jnp.einsum("kp,lpc->lkc", jnp.sin(yphase), columns, precision=HIGHEST_PREC)
    real_part = cos_part[:, :, 0::2] + sin_part[:, :, 1::2]
    imag_part = cos_part[:, :, 1::2] - sin_part[:, :, 0::2]
    return jnp.stack([real_part, imag_part], axis=-1).reshape(
        columns.shape[0], row_coord.shape[0], columns.shape[2]
    )


def shards(cell_ids, masses, block_dest, block_count, screen):
    size_x = lax.axis_size("px")
    size_y = lax.axis_size("py")
    devices = size_x * size_y
    num_planes = screen.shape[0]
    blocks = cell_ids.shape[0]
    block_size = cell_ids.shape[1]
    tile_rows = NY // size_x
    tile_cols = NZ // size_y
    row_share = tile_rows // size_y
    col_share = 2 * KZ // devices
    num_tiles = devices * num_planes
    dest_tile = block_dest[:, 0]
    places = lax.broadcasted_iota(jnp.int32, (blocks, block_size), 1)
    weight = jnp.where(places < block_count[:, None], masses, jnp.zeros_like(masses))
    order_row = lax.broadcasted_iota(jnp.int32, (blocks, blocks), 0)
    order_col = lax.broadcasted_iota(jnp.int32, (blocks, blocks), 1)
    before = (dest_tile[:, None] == dest_tile[None, :]) & (order_col < order_row)
    slot_rank = jnp.sum(before.astype(jnp.int32), axis=1)
    owner_dev = dest_tile // num_planes
    plane_of = dest_tile % num_planes
    slot_index = (plane_of * devices + owner_dev) * CAP + slot_rank
    send_cells = jnp.zeros((num_tiles * CAP, block_size), jnp.int32).at[slot_index].set(cell_ids)
    send_mass = jnp.zeros((num_tiles * CAP, block_size), jnp.bfloat16).at[slot_index].set(weight)
    num_slots = devices * CAP * block_size
    send_cells = send_cells.reshape(num_planes, devices, CAP, block_size)
    send_mass = send_mass.reshape(num_planes, devices, CAP, block_size)
    recv_cells, recv_mass = (
        lax.all_to_all(send_cells, ("px", "py"), split_axis=1, concat_axis=1, tiled=True),
        lax.all_to_all(send_mass, ("px", "py"), split_axis=1, concat_axis=1, tiled=True),
    )
    plane_cells = recv_cells.reshape(num_planes, num_slots)
    plane_mass = recv_mass.reshape(num_planes, num_slots)

    def deposit(packed):
        cell_row, mass_row = packed
        row_of = cell_row // tile_cols
        col_of = cell_row % tile_cols
        row_iota = lax.broadcasted_iota(jnp.int32, (num_slots, tile_rows), 1)
        col_iota = lax.broadcasted_iota(jnp.int32, (num_slots, tile_cols), 1)
        onehot_rows = (row_iota == row_of[:, None]).astype(jnp.bfloat16)
        mass_cols = jnp.where(
            col_iota == col_of[:, None], mass_row[:, None], jnp.zeros((), jnp.bfloat16)
        )
        return lax.dot_general(
            onehot_rows, mass_cols, (((0,), (0,)), ((), ())), preferred_element_type=jnp.float32
        )

    density = lax.map(deposit, (plane_cells, plane_mass))
    z_slab = lax.all_to_all(density, "py", split_axis=1, concat_axis=2, tiled=True)
    ztable = column_table(NZ)
    spectra = jnp.dot(
        z_slab.reshape(num_planes * row_share, NZ),
        ztable,
        precision=HIGHEST_PREC,
        preferred_element_type=jnp.float32,
    )
    spectra = spectra.reshape(num_planes, row_share, 2 * KZ)
    positions = lax.broadcasted_iota(jnp.int32, (KY, NY), 1)
    columns = lax.all_to_all(spectra, ("px", "py"), split_axis=2, concat_axis=1, tiled=True)
    mode_values = row_transform(positions, columns)
    device = lax.axis_index("px") * size_y + lax.axis_index("py")
    z_mode = (
        device * col_share + lax.broadcasted_iota(jnp.int32, (KY, col_share), 1)
    ) // 2 - KZ // 2
    y_mode = lax.broadcasted_iota(jnp.int32, (KY, col_share), 0) - KY // 2
    wave_sq = (2.0 * jnp.sin(math.pi * y_mode.astype(jnp.float32) / NY)) ** 2 + (
        2.0 * jnp.sin(math.pi * z_mode.astype(jnp.float32) / NZ)
    ) ** 2
    is_zero = (y_mode == 0) & (z_mode == 0)
    scr = screen[:, None, None]
    green_fn = jnp.where(is_zero[None], jnp.zeros_like(wave_sq)[None], -scr / (wave_sq[None] + scr))
    return mode_values * green_fn * (1.0 / math.sqrt(NY * NZ))


def solution(mesh):
    return jax.shard_map(
        shards,
        mesh=mesh,
        in_specs=(
            P(("px", "py"), None),
            P(("px", "py"), None),
            P(("px", "py"), None),
            P(("px", "py")),
            P(),
        ),
        out_specs=P(None, None, ("px", "py")),
        check_vma=False,
    )
```

profile of v0, /device:TPU:1, one launch (start us, length us, event | category | flops | bytes accessed | tf_op | source)
XLA Modules:
  0.0 397.6 jit_solution(6626434158525641063)
XLA Ops:
  0.0 1.3 convert_reduce_fusion
  2.0 4.2 %scatter_custom_fusion.1 = bf16[2048,128]{1,0:T(8,128)(2,1)S(1)} fusion(s32[1024]{0:T(1024)S(1)} %bitcast.66, bf16[1024,128]{1,0:T(8,128)(2,1)} %param.8, s32[1024]{0:T(1024)} %param.10, bf16[]{:T(256)} %constant.186.clone.1), kind=kCustom, calls=%fused_computation.71 | custom fusion | flops 262144 | bytes 791552 | tf_op jit(solution)/shard_map/scatter | solution.py:61
  7.3 11.5 %all-to-all-start.1 = ((bf16[8,128,2,128]{3,2,0,1:T(2,128)(2,1)}), bf16[8,128,2,128]{3,2,0,1:T(2,128)(2,1)S(1)}, u32[]{:S(2)}, u32[]{:S(2)}) async-start(bf16[8,128,2,128]{3,2,0,1:T(2,128)(2,1)} %copy.31), calls=%async_computation.1 | async-start | bytes 1048576 | tf_op jit(solution)/shard_map/all_to_all | solution.py:67
  18.8 3.7 scatter_custom_fusion
  22.6 1.3 copy.29
  23.9 8.8 %all-to-all-done.1 = bf16[8,128,2,128]{3,2,0,1:T(2,128)(2,1)S(1)} async-done(((bf16[8,128,2,128]{3,2,0,1:T(2,128)(2,1)}), bf16[8,128,2,128]{3,2,0,1:T(2,128)(2,1)S(1)}, u32[]{:S(2)}, u32[]{:S(2)}) %all-to-all-start.1) | async-done | bytes 524320 | tf_op jit(solution)/shard_map/all_to_all | solution.py:67
  32.7 4.2 %all-to-all-start = ((s32[8,128,2,128]{3,2,0,1:T(2,128)}), s32[8,128,2,128]{3,2,0,1:T(2,128)S(1)}, u32[]{:S(2)}, u32[]{:S(2)}) async-start(s32[8,128,2,128]{3,2,0,1:T(2,128)} %copy.29), calls=%async_computation | async-start | bytes 2097152 | tf_op jit(solution)/shard_map/all_to_all | solution.py:66
  38.5 17.5 %all-to-all-done = s32[8,128,2,128]{3,2,0,1:T(2,128)S(1)} async-done(((s32[8,128,2,128]{3,2,0,1:T(2,128)}), s32[8,128,2,128]{3,2,0,1:T(2,128)S(1)}, u32[]{:S(2)}, u32[]{:S(2)}) %all-to-all-start) | async-done | bytes 1048608 | tf_op jit(solution)/shard_map/all_to_all | solution.py:66
  57.2 279.6 %while.12 = (s32[]{:T(128)}, f32[8,256,128]{2,0,1:T(8,128)}, s32[8,32768]{1,0:T(8,128)S(1)}, bf16[8,32768]{1,0:T(8,128)(2,1)}, s32[]{:T(128)}, /*index=5*/s32[]{:T(128)}) while((s32[]{:T(128)}, f32[8,256,128]{2,0,1:T(8,128)}, s32[8,32768]{1,0:T(8,128)S(1)}, bf16[8,32768]{1,0:T(8,128)(2,1)}, s32[]{:T(128)}, /*index=5*/s32[]{:T(128)}) %tuple.34), condition=%wide.region_4.5_spmd, body=%wide.region_3.4_spmd.sunk | while | flops 2164883456 | bytes 18284624 | solution.py:86
  57.7 1.5 dynamic-slice_reduce_fusion.2
  59.1 12.0 %fusion.88 = bf16[32768,128]{1,0:T(8,128)(2,1)} fusion(s32[32768]{0:T(1024)S(1)} %get-tuple-element.110, bf16[32768]{0:T(1024)(128)(2,1)S(1)} %dynamic-slice_reduce_fusion.2), kind=kLoop, calls=%fused_computation.6.clone.clone.2.clone.1 | loop fusion | flops 8388608 | bytes 8585216 | tf_op jit(solution)/shard_map/while/body/eval_jaxpr/dot_general | solution.py:82
  71.1 16.6 %fusion.89 = f32[256,128]{1,0:T(8,128)S(1)} fusion(s32[32768]{0:T(1024)S(1)} %get-tuple-element.109, bf16[32768,128]{1,0:T(8,128)(2,1)} %fusion.88), kind=kOutput, calls=%fused_computation.3.clone.3 | convolution fusion | flops 2155872256 | bytes 8650752 | tf_op jit(solution)/shard_map/while/body/eval_jaxpr/dot_general | solution.py:82
  87.6 4.7 %dynamic_update_slice.8 = f32[8,256,128]{2,0,1:T(8,128)} dynamic-update-slice(f32[8,256,128]{2,0,1:T(8,128)} %get-tuple-element.118, f32[1,256,128]{2,0,1:T(1,128)S(1)} %bitcast.63, s32[]{:T(128)} %get-tuple-element.117, s32[]{:T(128)} %constant.176.clone.1..sunk, s32[]{:T(128)} %constant.176.clone.1..sunk) | dynamic-update-slice | bytes 262148 | tf_op jit(solution)/shard_map/while/body/jit(dynamic_update_index_in_dim)/dynamic_update_slice | solution.py:86
  92.5 1.5 dynamic-slice_reduce_fusion.2
  94.0 12.0 %fusion.88 = bf16[32768,128]{1,0:T(8,128)(2,1)} fusion(s32[32768]{0:T(1024)S(1)} %get-tuple-element.110, bf16[32768]{0:T(1024)(128)(2,1)S(1)} %dynamic-slice_reduce_fusion.2), kind=kLoop, calls=%fused_computation.6.clone.clone.2.clone.1 | loop fusion | flops 8388608 | bytes 8585216 | tf_op jit(solution)/shard_map/while/body/eval_jaxpr/dot_general | solution.py:82
  106.0 16.6 %fusion.89 = f32[256,128]{1,0:T(8,128)S(1)} fusion(s32[32768]{0:T(1024)S(1)} %get-tuple-element.109, bf16[32768,128]{1,0:T(8,128)(2,1)} %fusion.88), kind=kOutput, calls=%fused_computation.3.clone.3 | convolution fusion | flops 2155872256 | bytes 8650752 | tf_op jit(solution)/shard_map/while/body/eval_jaxpr/dot_general | solution.py:82
  122.5 4.7 %dynamic_update_slice.8 = f32[8,256,128]{2,0,1:T(8,128)} dynamic-update-slice(f32[8,256,128]{2,0,1:T(8,128)} %get-tuple-element.118, f32[1,256,128]{2,0,1:T(1,128)S(1)} %bitcast.63, s32[]{:T(128)} %get-tuple-element.117, s32[]{:T(128)} %constant.176.clone.1..sunk, s32[]{:T(128)} %constant.176.clone.1..sunk) | dynamic-update-slice | bytes 262148 | tf_op jit(solution)/shard_map/while/body/jit(dynamic_update_index_in_dim)/dynamic_update_slice | solution.py:86
  127.4 1.5 dynamic-slice_reduce_fusion.2
  128.9 12.0 %fusion.88 = bf16[32768,128]{1,0:T(8,128)(2,1)} fusion(s32[32768]{0:T(1024)S(1)} %get-tuple-element.110, bf16[32768]{0:T(1024)(128)(2,1)S(1)} %dynamic-slice_reduce_fusion.2), kind=kLoop, calls=%fused_computation.6.clone.clone.2.clone.1 | loop fusion | flops 8388608 | bytes 8585216 | tf_op jit(solution)/shard_map/while/body/eval_jaxpr/dot_general | solution.py:82
  140.8 16.6 %fusion.89 = f32[256,128]{1,0:T(8,128)S(1)} fusion(s32[32768]{0:T(1024)S(1)} %get-tuple-element.109, bf16[32768,128]{1,0:T(8,128)(2,1)} %fusion.88), kind=kOutput, calls=%fused_computation.3.clone.3 | convolution fusion | flops 2155872256 | bytes 8650752 | tf_op jit(solution)/shard_map/while/body/eval_jaxpr/dot_general | solution.py:82
  157.4 4.7 %dynamic_update_slice.8 = f32[8,256,128]{2,0,1:T(8,128)} dynamic-update-slice(f32[8,256,128]{2,0,1:T(8,128)} %get-tuple-element.118, f32[1,256,128]{2,0,1:T(1,128)S(1)} %bitcast.63, s32[]{:T(128)} %get-tuple-element.117, s32[]{:T(128)} %constant.176.clone.1..sunk, s32[]{:T(128)} %constant.176.clone.1..sunk) | dynamic-update-slice | bytes 262148 | tf_op jit(solution)/shard_map/while/body/jit(dynamic_update_index_in_dim)/dynamic_update_slice | solution.py:86
  162.3 1.5 dynamic-slice_reduce_fusion.2
  163.7 12.0 %fusion.88 = bf16[32768,128]{1,0:T(8,128)(2,1)} fusion(s32[32768]{0:T(1024)S(1)} %get-tuple-element.110, bf16[32768]{0:T(1024)(128)(2,1)S(1)} %dynamic-slice_reduce_fusion.2), kind=kLoop, calls=%fused_computation.6.clone.clone.2.clone.1 | loop fusion | flops 8388608 | bytes 8585216 | tf_op jit(solution)/shard_map/while/body/eval_jaxpr/dot_general | solution.py:82
  175.7 16.6 %fusion.89 = f32[256,128]{1,0:T(8,128)S(1)} fusion(s32[32768]{0:T(1024)S(1)} %get-tuple-element.109, bf16[32768,128]{1,0:T(8,128)(2,1)} %fusion.88), kind=kOutput, calls=%fused_computation.3.clone.3 | convolution fusion | flops 2155872256 | bytes 8650752 | tf_op jit(solution)/shard_map/while/body/eval_jaxpr/dot_general | solution.py:82
  192.3 4.7 %dynamic_update_slice.8 = f32[8,256,128]{2,0,1:T(8,128)} dynamic-update-slice(f32[8,256,128]{2,0,1:T(8,128)} %get-tuple-element.118, f32[1,256,128]{2,0,1:T(1,128)S(1)} %bitcast.63, s32[]{:T(128)} %get-tuple-element.117, s32[]{:T(128)} %constant.176.clone.1..sunk, s32[]{:T(128)} %constant.176.clone.1..sunk) | dynamic-update-slice | bytes 262148 | tf_op jit(solution)/shard_map/while/body/jit(dynamic_update_index_in_dim)/dynamic_update_slice | solution.py:86
  197.2 1.5 dynamic-slice_reduce_fusion.2
  198.6 12.0 %fusion.88 = bf16[32768,128]{1,0:T(8,128)(2,1)} fusion(s32[32768]{0:T(1024)S(1)} %get-tuple-element.110, bf16[32768]{0:T(1024)(128)(2,1)S(1)} %dynamic-slice_reduce_fusion.2), kind=kLoop, calls=%fused_computation.6.clone.clone.2.clone.1 | loop fusion | flops 8388608 | bytes 8585216 | tf_op jit(solution)/shard_map/while/body/eval_jaxpr/dot_general | solution.py:82
  210.6 16.6 %fusion.89 = f32[256,128]{1,0:T(8,128)S(1)} fusion(s32[32768]{0:T(1024)S(1)} %get-tuple-element.109, bf16[32768,128]{1,0:T(8,128)(2,1)} %fusion.88), kind=kOutput, calls=%fused_computation.3.clone.3 | convolution fusion | flops 2155872256 | bytes 8650752 | tf_op jit(solution)/shard_map/while/body/eval_jaxpr/dot_general | solution.py:82
  227.2 4.7 %dynamic_update_slice.8 = f32[8,256,128]{2,0,1:T(8,128)} dynamic-update-slice(f32[8,256,128]{2,0,1:T(8,128)} %get-tuple-element.118, f32[1,256,128]{2,0,1:T(1,128)S(1)} %bitcast.63, s32[]{:T(128)} %get-tuple-element.117, s32[]{:T(128)} %constant.176.clone.1..sunk, s32[]{:T(128)} %constant.176.clone.1..sunk) | dynamic-update-slice | bytes 262148 | tf_op jit(solution)/shard_map/while/body/jit(dynamic_update_index_in_dim)/dynamic_update_slice | solution.py:86
  232.1 1.5 dynamic-slice_reduce_fusion.2
  233.5 12.0 %fusion.88 = bf16[32768,128]{1,0:T(8,128)(2,1)} fusion(s32[32768]{0:T(1024)S(1)} %get-tuple-element.110, bf16[32768]{0:T(1024)(128)(2,1)S(1)} %dynamic-slice_reduce_fusion.2), kind=kLoop, calls=%fused_computation.6.clone.clone.2.clone.1 | loop fusion | flops 8388608 | bytes 8585216 | tf_op jit(solution)/shard_map/while/body/eval_jaxpr/dot_general | solution.py:82
  245.5 16.6 %fusion.89 = f32[256,128]{1,0:T(8,128)S(1)} fusion(s32[32768]{0:T(1024)S(1)} %get-tuple-element.109, bf16[32768,128]{1,0:T(8,128)(2,1)} %fusion.88), kind=kOutput, calls=%fused_computation.3.clone.3 | convolution fusion | flops 2155872256 | bytes 8650752 | tf_op jit(solution)/shard_map/while/body/eval_jaxpr/dot_general | solution.py:82
  262.0 4.7 %dynamic_update_slice.8 = f32[8,256,128]{2,0,1:T(8,128)} dynamic-update-slice(f32[8,256,128]{2,0,1:T(8,128)} %get-tuple-element.118, f32[1,256,128]{2,0,1:T(1,128)S(1)} %bitcast.63, s32[]{:T(128)} %get-tuple-element.117, s32[]{:T(128)} %constant.176.clone.1..sunk, s32[]{:T(128)} %constant.176.clone.1..sunk) | dynamic-update-slice | bytes 262148 | tf_op jit(solution)/shard_map/while/body/jit(dynamic_update_index_in_dim)/dynamic_update_slice | solution.py:86
  266.9 1.5 dynamic-slice_reduce_fusion.2
  268.4 12.0 %fusion.88 = bf16[32768,128]{1,0:T(8,128)(2,1)} fusion(s32[32768]{0:T(1024)S(1)} %get-tuple-element.110, bf16[32768]{0:T(1024)(128)(2,1)S(1)} %dynamic-slice_reduce_fusion.2), kind=kLoop, calls=%fused_computation.6.clone.clone.2.clone.1 | loop fusion | flops 8388608 | bytes 8585216 | tf_op jit(solution)/shard_map/while/body/eval_jaxpr/dot_general | solution.py:82
  280.4 16.6 %fusion.89 = f32[256,128]{1,0:T(8,128)S(1)} fusion(s32[32768]{0:T(1024)S(1)} %get-tuple-element.109, bf16[32768,128]{1,0:T(8,128)(2,1)} %fusion.88), kind=kOutput, calls=%fused_computation.3.clone.3 | convolution fusion | flops 2155872256 | bytes 8650752 | tf_op jit(solution)/shard_map/while/body/eval_jaxpr/dot_general | solution.py:82
  296.9 4.7 %dynamic_update_slice.8 = f32[8,256,128]{2,0,1:T(8,128)} dynamic-update-slice(f32[8,256,128]{2,0,1:T(8,128)} %get-tuple-element.118, f32[1,256,128]{2,0,1:T(1,128)S(1)} %bitcast.63, s32[]{:T(128)} %get-tuple-element.117, s32[]{:T(128)} %constant.176.clone.1..sunk, s32[]{:T(128)} %constant.176.clone.1..sunk) | dynamic-update-slice | bytes 262148 | tf_op jit(solution)/shard_map/while/body/jit(dynamic_update_index_in_dim)/dynamic_update_slice | solution.py:86
  301.8 1.5 dynamic-slice_reduce_fusion.2
  303.3 12.0 %fusion.88 = bf16[32768,128]{1,0:T(8,128)(2,1)} fusion(s32[32768]{0:T(1024)S(1)} %get-tuple-element.110, bf16[32768]{0:T(1024)(128)(2,1)S(1)} %dynamic-slice_reduce_fusion.2), kind=kLoop, calls=%fused_computation.6.clone.clone.2.clone.1 | loop fusion | flops 8388608 | bytes 8585216 | tf_op jit(solution)/shard_map/while/body/eval_jaxpr/dot_general | solution.py:82
  315.2 16.6 %fusion.89 = f32[256,128]{1,0:T(8,128)S(1)} fusion(s32[32768]{0:T(1024)S(1)} %get-tuple-element.109, bf16[32768,128]{1,0:T(8,128)(2,1)} %fusion.88), kind=kOutput, calls=%fused_computation.3.clone.3 | convolution fusion | flops 2155872256 | bytes 8650752 | tf_op jit(solution)/shard_map/while/body/eval_jaxpr/dot_general | solution.py:82
  331.8 4.7 %dynamic_update_slice.8 = f32[8,256,128]{2,0,1:T(8,128)} dynamic-update-slice(f32[8,256,128]{2,0,1:T(8,128)} %get-tuple-element.118, f32[1,256,128]{2,0,1:T(1,128)S(1)} %bitcast.63, s32[]{:T(128)} %get-tuple-element.117, s32[]{:T(128)} %constant.176.clone.1..sunk, s32[]{:T(128)} %constant.176.clone.1..sunk) | dynamic-update-slice | bytes 262148 | tf_op jit(solution)/shard_map/while/body/jit(dynamic_update_index_in_dim)/dynamic_update_slice | solution.py:86
  336.9 3.7 all-to-all-start.2
  340.8 15.1 %all-to-all-done.2 = f32[8,256,128]{2,0,1:T(8,128)S(1)} async-done(((f32[8,256,128]{2,0,1:T(8,128)}), f32[8,256,128]{2,0,1:T(8,128)S(1)}, u32[]{:S(2)}, u32[]{:S(2)}) %all-to-all-start.2) | async-done | bytes 1048608 | tf_op jit(solution)/shard_map/all_to_all | solution.py:87
  356.6 9.5 %fusion.14 = f32[8,16,256]{2,1,0:T(8,128)S(1)} fusion(f32[8,16,2048]{2,1,0:T(8,128)S(1)} %dot_general.17, s32[256]{0:T(256)S(1)} %get-tuple-element.74, s32[256]{0:T(256)S(1)} %get-tuple-element.79, s32[256]{0:T(256)S(1)} %get-tuple-element.75, s32[256]{0:T(256)S(1)} %get-tuple-element.78, pred[256]{0:T(512)(128)(4,1)S(1)} %get-tuple-element.76, ...), kind=kOutput, calls=%fused_computation.30 | convolution fusion | flops 815792128 | bytes 1184256 | tf_op jit(solution)/shard_map/dot_general | solution.py:89
  367.6 6.7 %all-to-all-start.3 = ((f32[128,1,256]{2,1,0:T(1,128)}), f32[128,1,256]{2,1,0:T(1,128)S(1)}, u32[]{:S(2)}, u32[]{:S(2)}) async-start(f32[128,1,256]{2,1,0:T(1,128)} %reshape.223), calls=%async_computation.3 | async-start | bytes 262144 | tf_op jit(solution)/shard_map/all_to_all | solution.py:97
  374.4 10.0 %all-to-all-done.3 = f32[128,1,256]{2,1,0:T(1,128)S(1)} async-done(((f32[128,1,256]{2,1,0:T(1,128)}), f32[128,1,256]{2,1,0:T(1,128)S(1)}, u32[]{:S(2)}, u32[]{:S(2)}) %all-to-all-start.3) | async-done | bytes 131104 | tf_op jit(solution)/shard_map/all_to_all | solution.py:97
  387.3 4.7 %convolution_bitcast_fusion = f32[8,128,2]{1,0,2:T(8,128)S(1)} fusion(f32[8,2048,2]{1,0,2:T(8,128)S(1)} %all_to_all.38, s32[128]{0:T(128)S(1)} %iota_add_fusion.1), kind=kOutput, calls=%fused_computation.43 | convolution fusion | flops 54001664 | bytes 139776 | tf_op jit(solution)/shard_map/kp,lpc->lkc/dot_general | solution.py:30
  392.0 4.7 %convolution_bitcast_fusion.1 = f32[8,128,2]{1,0,2:T(8,128)S(1)} fusion(f32[8,2048,2]{1,0,2:T(8,128)S(1)} %all_to_all.38, s32[128]{0:T(128)S(1)} %iota_add_fusion.1), kind=kOutput, calls=%fused_computation.44 | convolution fusion | flops 54001664 | bytes 139776 | tf_op jit(solution)/shard_map/kp,lpc->lkc/dot_general | solution.py:29
  (48 shorter events, 12.3 us)
Async XLA Ops:
  7.3 25.4 %all-to-all-start.1 = ((bf16[8,128,2,128]{3,2,0,1:T(2,128)(2,1)}), bf16[8,128,2,128]{3,2,0,1:T(2,128)(2,1)S(1)}, u32[]{:S(2)}, u32[]{:S(2)}) async-start(bf16[8,128,2,128]{3,2,0,1:T(2,128)(2,1)} %copy.31), calls=%async_computation.1 | async-start | bytes 1048576 | tf_op jit(solution)/shard_map/all_to_all | solution.py:67
  32.7 23.3 %all-to-all-start = ((s32[8,128,2,128]{3,2,0,1:T(2,128)}), s32[8,128,2,128]{3,2,0,1:T(2,128)S(1)}, u32[]{:S(2)}, u32[]{:S(2)}) async-start(s32[8,128,2,128]{3,2,0,1:T(2,128)} %copy.29), calls=%async_computation | async-start | bytes 2097152 | tf_op jit(solution)/shard_map/all_to_all | solution.py:66
  336.9 19.0 %all-to-all-start.2 = ((f32[8,256,128]{2,0,1:T(8,128)}), f32[8,256,128]{2,0,1:T(8,128)S(1)}, u32[]{:S(2)}, u32[]{:S(2)}) async-start(f32[8,256,128]{2,0,1:T(8,128)} %get-tuple-element.61), calls=%async_computation.2 | async-start | bytes 2097152 | tf_op jit(solution)/shard_map/all_to_all | solution.py:87
  366.2 8.2 %copy-start = (f32[8]{0:T(128)S(1)}, f32[8]{0:T(128)}, u32[]{:S(2)}) copy-start(f32[8]{0:T(128)} %param.11) | copy-start | bytes 100
  367.6 16.8 %all-to-all-start.3 = ((f32[128,1,256]{2,1,0:T(1,128)}), f32[128,1,256]{2,1,0:T(1,128)S(1)}, u32[]{:S(2)}, u32[]{:S(2)}) async-start(f32[128,1,256]{2,1,0:T(1,128)} %reshape.223), calls=%async_computation.3 | async-start | bytes 262144 | tf_op jit(solution)/shard_map/all_to_all | solution.py:97
where the time goes:
time: 405 us; the launch traced here: 398 us
  matrix products  151 us (37%)
  other arithmetic  104 us (26%)
  local copies, waits for them, and re-layouts  63.4 us (16%)
  waiting for transfers between devices  51.4 us (13%)
  starting transfers between devices  26.1 us (6%)
    dot_general x8, matrix products, deposit(): lax.dot_general(onehot_rows, mass_cols, (((0,), (0,)), ((), ())), preferr...  132 us
    dot_general x8, other arithmetic, deposit(): lax.dot_general(onehot_rows, mass_cols, (((0,), (0,)), ((), ())), preferr...  95.8 us
    dynamic_update_slice x8, local copies, waits for them, and re-layouts, shards(): density = lax.map(deposit, (plane_cells, plane_mass))  37.4 us
    all_to_all x1, waiting for transfers between devices, shards(): lax.all_to_all(send_cells, ('px', 'py'), split_axis=1, concat_axis=1, til...  17.5 us
    all_to_all x1, waiting for transfers between devices, shards(): lax.all_to_all(density, 'py', split_axis=1, concat_axis=2, tiled=True)  15.1 us
    dynamic_slice x16, local copies, waits for them, and re-layouts, shards(): density = lax.map(deposit, (plane_cells, plane_mass))  12.4 us
    all_to_all x1, starting transfers between devices, shards(): lax.all_to_all(send_mass, ('px', 'py'), split_axis=1, concat_axis=1, tile...  11.5 us
    all_to_all x1, waiting for transfers between devices, shards(): lax.all_to_all(spectra, ('px', 'py'), split_axis=2, concat_axis=1, tiled=...  10 us
  transfers between devices with their start and end apart: 4, of which 4 were waited for; matrix products, arithmetic and copies ran while one was open for 2% of the time, Pallas kernels for 0%

commit v1 on v0

v1 whole, which is shorter than its diff:
```python
import math

import jax
import jax.numpy as jnp
import numpy as np
from jax import lax
from jax.experimental import pallas as pl
from jax.experimental.pallas import tpu as pltpu
from jax.sharding import PartitionSpec as P

NY = 2048
NZ = 2048
PL = 8
KY = 128
KZ = 128
N_PY = 16
SUB = 128
Q = 32
UNROLL = 16


def polynomial_table():
    x = (np.arange(SUB) - (SUB - 1) / 2) / (SUB / 2)
    return np.cos(np.arange(Q)[:, None] * np.arccos(x)[None, :])


def twiddle_factors(length):
    freqs = np.arange(128) - 64
    angle = 2.0 * np.pi * freqs / length
    nodes = (np.arange(512) + 0.5) * np.pi / 512
    waves = np.exp(-1j * (angle * SUB / 2)[:, None] * np.cos(nodes)[None, :])
    coefs = (2.0 / 512) * waves @ np.cos(nodes[:, None] * np.arange(Q)[None, :])
    coefs[:, 0] /= 2
    starts = np.arange(length // SUB) * SUB + (SUB - 1) / 2
    shift = np.exp(-1j * starts[:, None] * angle[None, :])
    return shift[:, None, :] * coefs.T[None, :, :]


def block_kernel(dest_ref, count_ref, table_ref, cells_ref, mass_ref, out_ref):
    out_ref[...] = jnp.zeros_like(out_ref)
    lane = lax.broadcasted_iota(jnp.int32, (1, SUB), 1)

    def step(group, carry):
        base = pl.multiple_of(group * UNROLL, UNROLL)
        cells = cells_ref[pl.ds(base, UNROLL), :]
        mass = mass_ref[pl.ds(base, UNROLL), :].astype(jnp.float32)
        table = table_ref[...]
        for j in range(UNROLL):
            tile = dest_ref[base + j]
            count = count_ref[base + j]
            plane = tile % PL
            device = tile // PL
            tile_row = device // N_PY
            tile_col = device % N_PY
            cell = cells[j : j + 1, :]
            w = jnp.where(lane < count, mass[j : j + 1, :], 0.0)
            z_at = jnp.broadcast_to(cell & (SUB - 1), (Q, SUB))
            y_at = jnp.broadcast_to((cell >> 7) & (SUB - 1), (Q, SUB))
            quarter = (cell >> 14) + 2 * (tile_row % 2)
            z = jnp.take_along_axis(table, z_at, axis=1) * w
            y = jnp.take_along_axis(table, y_at, axis=1)
            z_hi = z.astype(jnp.bfloat16)
            z_lo = (z - z_hi.astype(jnp.float32)).astype(jnp.bfloat16)
            y_hi = y.astype(jnp.bfloat16)
            y_lo = (y - y_hi.astype(jnp.float32)).astype(jnp.bfloat16)
            picks = [(quarter == k).astype(jnp.float32).astype(jnp.bfloat16) for k in range(4)]
            y_hi = jnp.concatenate([y_hi * pick for pick in picks], axis=0)
            y_lo = jnp.concatenate([y_lo * pick for pick in picks], axis=0)
            left = jnp.concatenate([z_hi, z_hi, z_lo], axis=1)
            right = jnp.concatenate([y_hi, y_lo, y_hi], axis=1)
            part = lax.dot_general(
                left, right, (((1,), (1,)), ((), ())), preferred_element_type=jnp.float32
            )
            row = pl.multiple_of((plane * N_PY + tile_col) * Q, Q)
            out_ref[tile_row // 2, pl.ds(row, Q), :] += part
        return carry

    lax.fori_loop(0, cells_ref.shape[0] // UNROLL, step, 0)


def block_sums(dest, count, table, cells, mass):
    rows = PL * N_PY * Q
    return pl.pallas_call(
        block_kernel,
        out_shape=jax.ShapeDtypeStruct((4, rows, SUB), jnp.float32),
        in_specs=[pl.BlockSpec(memory_space=pltpu.SMEM)] * 2
        + [pl.BlockSpec(memory_space=pltpu.VMEM)] * 3,
        out_specs=pl.BlockSpec(memory_space=pltpu.VMEM),
        compiler_params=pltpu.CompilerParams(vmem_limit_bytes=48 << 20),
    )(dest, count, table, cells, mass)


def shards(cell_ids, masses, block_dest, block_count, screen):
    table = jnp.asarray(polynomial_table(), jnp.float32)
    sums = block_sums(block_dest[:, 0], block_count, table, cell_ids, masses)
    grid = sums.reshape(4, PL, N_PY * Q, SUB)
    z_factors = twiddle_factors(NZ).reshape(N_PY * Q, KZ)
    y_factors = twiddle_factors(NY).reshape(4, SUB, KY)
    z_side = jnp.asarray(np.stack([z_factors.real, z_factors.imag]), jnp.float32)
    y_cos = jnp.asarray(np.stack([y_factors.real, y_factors.imag]), jnp.float32)
    y_sin = jnp.asarray(np.stack([-y_factors.imag, y_factors.real]), jnp.float32)
    exact = lax.Precision.HIGHEST
    half = jnp.einsum("czn,ipzl->cpnil", z_side, grid, precision=exact)
    partial = jnp.einsum("pnil,cilm->npcm", half[0], y_cos, precision=exact)
    partial += jnp.einsum("pnil,cilm->npcm", half[1], y_sin, precision=exact)
    total = lax.psum_scatter(partial, ("px", "py"), scatter_dimension=0, tiled=True)[0]
    device = lax.axis_index("px") * lax.axis_size("py") + lax.axis_index("py")
    z_freq = (device - KZ // 2).astype(jnp.float32)
    y_freq = (lax.broadcasted_iota(jnp.int32, (1, KY), 1) - KY // 2).astype(jnp.float32)
    wave_sq = (2.0 * jnp.sin(math.pi * y_freq / NY)) ** 2 + (
        2.0 * jnp.sin(math.pi * z_freq / NZ)
    ) ** 2
    scr = screen[:, None]
    green = jnp.where((y_freq == 0.0) & (z_freq == 0.0), 0.0, -scr / (wave_sq + scr))
    modes = total * green[:, None, :] * (1.0 / math.sqrt(NY * NZ))
    return jnp.swapaxes(modes, 1, 2)


def solution(mesh):
    return jax.shard_map(
        shards,
        mesh=mesh,
        in_specs=(
            P(("px", "py"), None),
            P(("px", "py"), None),
            P(("px", "py"), None),
            P(("px", "py")),
            P(),
        ),
        out_specs=P(None, None, ("px", "py")),
        check_vma=False,
    )
```

time: 405 us -> 739 us (1.82)
  the two profiles are of different devices: /device:TPU:1 before, /device:TPU:0 now
where the time goes in v1:
time: 739 us; the launch traced here: 738 us
  waiting for transfers between devices  642 us (87%)
  Pallas kernels  52.3 us (7%)
  matrix products  22.8 us (3%)
  between operations  13.6 us (2%)
    reduce_scatter x1, waiting for transfers between devices, shards(): lax.psum_scatter(partial, ('px', 'py'), scatter_dimension=0, tiled=True)[0]  642 us
    pallas_call x1, Pallas kernels, block_sums(): pl.pallas_call(block_kernel, out_shape=jax.ShapeDtypeStruct((4, rows, SUB...  52.3 us
    dot_general x1, matrix products, shards(): half = jnp.einsum('czn,ipzl->cpnil', z_side, grid, precision=exact)  15.9 us
  transfers between devices with their start and end apart: 1, of which 1 were waited for; matrix products, arithmetic and copies ran while one was open for 0% of the time, Pallas kernels for 0%

profile of v1, /device:TPU:0, one launch (start us, length us, event | category | flops | bytes accessed | tf_op | source)
XLA Modules:
  0.0 738.4 jit_solution(15683419397728337586)
XLA Ops:
  6.5 0.0 reduce-scatter.2.cloned.1.call-start
  6.5 0.0 copy-start
  6.5 1.0 copy-done
  7.6 0.0 copy-start.1
  7.6 0.9 copy-done.1
  8.5 0.0 copy-start.2
  8.5 0.7 copy-done.2
  9.2 0.0 copy-start.3
  9.2 0.7 copy-done.3
  9.9 0.0 copy-start.4
  9.9 0.7 copy-done.4
  10.6 0.0 copy-start.7
  10.6 52.3 %shard_map.91 = f32[4,4096,128]{2,1,0:T(8,128)} custom-call(s32[1024]{0:T(1024)S(1)} %bitcast.45, s32[1024]{0:T(1024)S(1)} %copy-done.4, f32[32,128]{1,0:T(8,128)S(1)} %copy-done.2, s32[1024,128]{1,0:T(8,128)S(1)} %copy-done, bf16[1024,128]{1,0:T(8,128)(2,1)S(1)} %copy-done.1), custom_call_target="tpu_custom_call" | custom-call | tf_op jit(solution)/shard_map/pallas_call | solution.py:83
  62.9 0.0 copy-done.7
  62.9 15.9 %convolution_bitcast_fusion = f32[2,8,128,4,128]{2,4,0,1,3:T(8,128)S(1)} fusion(f32[4,8,512,128,1]{3,2,4,1,0:T(8,128)} %bitcast.46, f32[2,512,128,1,1]{2,1,0,4,3:T(8,128)S(1)} %copy-done.7), kind=kOutput, calls=%fused_computation | convolution fusion | flops 6442450944 | bytes 13107200 | tf_op jit(solution)/shard_map/czn,ipzl->cpnil/dot_general | solution.py:103
  78.8 0.0 copy-start.6
  78.8 0.5 slice_bitcast_fusion
  79.3 0.0 copy-start.5
  79.3 0.5 copy-done.6
  79.9 3.4 fusion.4
  83.3 0.0 copy-done.5
  83.3 3.5 fusion.13
  86.8 0.0 copy-start.8
  86.8 1.6 copy.16
  88.4 0.0 reduce-scatter.2.cloned.1.call-update
  88.5 0.0 copy-done.8
  88.6 0.1 divide_select_fusion
  88.7 641.6 %reduce-scatter.2.cloned.1.call-done = f32[1,8,2,128]{3,1,2,0:T(8,128)} async-done(((f32[128,8,2,128]{3,1,2,0:T(8,128)}), f32[1,8,2,128]{3,1,2,0:T(8,128)}) %reduce-scatter.2.cloned.1.call-update) | async-done | bytes 8208 | tf_op jit(solution)/shard_map/reduce_scatter | solution.py:106
  730.3 0.7 fusion.17
  731.0 0.6 copy.17
  (3 shorter events, 0.1 us)
Async XLA Ops:
  6.5 723.7 %reduce-scatter.2.cloned.1.call-start = ((), (), s32[]{:S(2)}) async-start(), calls=%async_computation.1 | async-start | bytes 1056768 | tf_op jit(solution)/shard_map/reduce_scatter | solution.py:106
  6.5 1.0 copy-start
  7.6 0.9 copy-start.1
  8.5 0.7 copy-start.2
  9.2 0.7 copy-start.3
  9.9 0.7 copy-start.4
  10.6 52.3 %copy-start.7 = (f32[2,512,128,1,1]{2,1,0,4,3:T(8,128)S(1)}, f32[2,512,128,1,1]{2,1,0,4,3:T(8,128)}, u32[]{:S(2)}) copy-start(f32[2,512,128,1,1]{2,1,0,4,3:T(8,128)} %constant.47) | copy-start | bytes 1572868
  78.8 1.0 copy-start.6
  79.3 4.0 copy-start.5
  86.8 1.7 copy-start.8
Sparse Core Ops, SparseCore 0:
  88.5 641.6 reduce-scatter.1

commit v2 on v1

v2 whole, which is shorter than its diff:
```python
import math

import jax
import jax.numpy as jnp
import ml_dtypes
import numpy as np
from jax import lax
from jax.experimental import pallas as pl
from jax.experimental.pallas import tpu as pltpu
from jax.sharding import PartitionSpec as P

NY = 2048
NZ = 2048
PL = 8
KY = 128
KZ = 128
N_PX = 8
N_PY = 16
DEVICES = N_PX * N_PY
SUB = 128
Q = 32
UNROLL = 64
SPAN = N_PY * Q
HALF = 72
PARTS = 2 * PL
SLOTS = 129

MESH = pl.DeviceIdType.MESH


def twiddle_factors(freqs, length):
    angle = 2.0 * np.pi * freqs / length
    nodes = (np.arange(512) + 0.5) * np.pi / 512
    waves = np.exp(-1j * (angle * SUB / 2)[:, None] * np.cos(nodes)[None, :])
    coefs = (2.0 / 512) * waves @ np.cos(nodes[:, None] * np.arange(Q)[None, :])
    coefs[:, 0] /= 2
    starts = np.arange(length // SUB) * SUB + (SUB - 1) / 2
    shift = np.exp(-1j * starts[:, None] * angle[None, :])
    return (shift[:, None, :] * coefs.T[None, :, :]).reshape(-1, len(freqs))


def two_parts(values):
    high = values.astype(ml_dtypes.bfloat16)
    low = (values - high.astype(np.float64)).astype(ml_dtypes.bfloat16)
    return high, low


def z_table():
    factors = twiddle_factors(np.arange(HALF) * (np.arange(HALF) <= 64), NZ)
    return np.concatenate(two_parts(np.concatenate([factors.real, factors.imag], axis=1).T))


def y_table():
    factors = twiddle_factors(np.arange(KY) - KY // 2, NY)
    real, imag = factors.real, factors.imag
    both = np.stack(
        [np.concatenate([real, imag], axis=1), np.concatenate([-imag, real], axis=1)]
    )
    return np.stack(two_parts(both))


def split(values):
    high = values.astype(jnp.bfloat16)
    return high, (values - high.astype(jnp.float32)).astype(jnp.bfloat16)


def dot(a, b):
    return jnp.dot(a, b, preferred_element_type=jnp.float32)


def chain(ref, first, x):
    twice = x + x
    before, now = first, first * x
    ref[0:8, :] = before
    ref[8:16, :] = now
    for q in range(2, Q):
        before, now = now, twice * now - before
        ref[8 * q : 8 * q + 8, :] = now


def block_kernel(dest_ref, count_ref, cells_ref, mass_ref, z_ref, y_ref, out_ref, sums, half, *chains):
    sums[...] = jnp.zeros_like(sums)
    lane = lax.broadcasted_iota(jnp.int32, (8, SUB), 1)
    upper = lax.broadcasted_iota(jnp.int32, (Q, SUB), 1) >= SUB // 2

    def step(group, carry):
        none = jnp.zeros((Q, SUB), jnp.bfloat16)
        first = pl.multiple_of(group * UNROLL, UNROLL)
        masses = mass_ref[pl.ds(first, UNROLL), :].astype(jnp.float32)
        for eight in range(UNROLL // 8):
            z_chain, y_chain = chains[2 * eight], chains[2 * eight + 1]
            base = pl.multiple_of(first + 8 * eight, 8)
            cells = cells_ref[pl.ds(base, 8), :]
            live = lane < count_ref[pl.ds(base, 8), :]
            weight = jnp.where(live, masses[8 * eight : 8 * eight + 8], 0.0)
            z_at = ((cells & (SUB - 1)).astype(jnp.float32) - (SUB - 1) / 2) * (2 / SUB)
            y_at = (((cells >> 7) & (SUB - 1)).astype(jnp.float32) - (SUB - 1) / 2) * (2 / SUB)
            chain(z_chain, weight, z_at)
            chain(y_chain, jnp.ones_like(weight), y_at)
            lower_half = (cells >> 14).astype(jnp.float32)
            for pair in range(0, 8, 2):
                left, right = [], []
                for j in (pair, pair + 1):
                    rows = [pl.ds(64 * i + j, 8, stride=8) for i in range(Q // 8)]
                    left.append(split(jnp.concatenate([z_chain[r, :] for r in rows], axis=0)))
                    high, low = split(jnp.concatenate([y_chain[r, :] for r in rows], axis=0))
                    second = lower_half[j : j + 1]
                    first_half = (1.0 - second).astype(jnp.bfloat16)
                    second = second.astype(jnp.bfloat16)
                    right.append(
                        jnp.concatenate(
                            [high * first_half, high * second, low * first_half, low * second],
                            axis=0,
                        )
                    )
                left = jnp.concatenate(
                    [
                        jnp.concatenate([left[0][0], left[0][1], none, none], axis=0),
                        jnp.concatenate([none, none, left[1][0], left[1][1]], axis=0),
                    ],
                    axis=1,
                )
                part = lax.dot_general(
                    left,
                    jnp.concatenate(right, axis=1),
                    (((1,), (1,)), ((), ())),
                    preferred_element_type=jnp.float32,
                )
                for j in range(2):
                    tile = dest_ref[base + pair + j]
                    plane, device = tile & (PL - 1), tile >> 3
                    tile_row, tile_col = device >> 4, device & (N_PY - 1)
                    block = part[64 * j : 64 * j + 32] + part[64 * j + 32 : 64 * j + 64]
                    block = block + pltpu.roll(block, SUB // 2, 1)
                    block = jnp.where(upper == ((tile_row & 1) == 1), block, 0.0)
                    row = pl.multiple_of((plane * N_PY + tile_col) * Q, Q)
                    sums[tile_row >> 1, pl.ds(row, Q), :] += block
        return carry

    lax.fori_loop(0, cells_ref.shape[0] // UNROLL, step, 0)

    def transform(plane, carry):
        row = pl.multiple_of(plane * SPAN, SPAN)
        for i in range(4):
            high, low = split(sums[i, pl.ds(row, SPAN), :])
            product = dot(z_ref[0 : 2 * HALF, :], jnp.concatenate([high, low], axis=1))
            product = product[:, :SUB] + product[:, SUB:]
            product += dot(z_ref[2 * HALF :, :], high)
            half[:, SUB * i : SUB * i + SUB] = product
        modes = []
        for c in range(2):
            high, low = split(half[HALF * c : HALF * c + HALF, :])
            modes.append(
                dot(high, y_ref[0, c]) + dot(low, y_ref[0, c]) + dot(high, y_ref[1, c])
            )
        plus, minus = modes[0] + modes[1], modes[0] - modes[1]
        for c in range(2):
            lanes = slice(KY * c, KY * c + KY)
            at = PL * c + plane
            out_ref[pl.ds(at, 64, stride=PARTS), :] = plus[0:64, lanes]
            out_ref[pl.ds(64 * PARTS + at, 65, stride=PARTS), :] = minus[0:65, lanes]
        return carry

    lax.fori_loop(0, PL, transform, 0)


def partial_modes(dest, count, cells, mass):
    blocks = cells.shape[0]
    counts = jnp.broadcast_to(count[:, None], (blocks, SUB))
    return pl.pallas_call(
        block_kernel,
        out_shape=jax.ShapeDtypeStruct((SLOTS * PARTS, KY), jnp.float32),
        in_specs=[pl.BlockSpec(memory_space=pltpu.SMEM)]
        + [pl.BlockSpec(memory_space=pltpu.VMEM)] * 5,
        out_specs=pl.BlockSpec(memory_space=pltpu.VMEM),
        scratch_shapes=[
            pltpu.VMEM((4, PL * SPAN, SUB), jnp.float32),
            pltpu.VMEM((2 * HALF, SPAN), jnp.float32),
        ]
        + [pltpu.VMEM((Q * 8, SUB), jnp.float32)] * (UNROLL // 4),
        compiler_params=pltpu.CompilerParams(vmem_limit_bytes=48 << 20),
    )(dest, counts, cells, mass, jnp.asarray(z_table()), jnp.asarray(y_table()))


def position():
    return lax.axis_index("px") * N_PY + lax.axis_index("py")


def slot_of(device):
    ahead = device // 64
    return ahead * (device - 64) + (1 - ahead) * (128 - device)


def exchange_kernel(part_ref, green_ref, out_ref, landed, send_sem, recv_sem):
    me = position()
    barrier = pltpu.get_barrier_semaphore()

    def greet(k, carry):
        to = lax.rem(me + k, DEVICES)
        pl.semaphore_signal(barrier, inc=1, device_id=(to // N_PY, to % N_PY), device_id_type=MESH)
        return carry

    lax.fori_loop(1, DEVICES, greet, 0)
    pl.semaphore_wait(barrier, DEVICES - 1)

    def send(k, carry):
        to = lax.rem(me + k, DEVICES)
        pltpu.make_async_remote_copy(
            src_ref=part_ref.at[pl.ds(pl.multiple_of(slot_of(to) * PARTS, PARTS), PARTS)],
            dst_ref=landed.at[pl.ds(pl.multiple_of((k - 1) * PARTS, PARTS), PARTS)],
            send_sem=send_sem,
            recv_sem=recv_sem,
            device_id=(to // N_PY, to % N_PY),
            device_id_type=MESH,
        ).start()
        return carry

    lax.fori_loop(1, DEVICES, send, 0)
    pltpu.make_async_copy(landed, landed, recv_sem).wait()
    total = part_ref[pl.ds(pl.multiple_of(slot_of(me) * PARTS, PARTS), PARTS), :]
    parts = landed[...].reshape(DEVICES - 1, PARTS, KY)
    out_ref[...] = (total + jnp.sum(parts, axis=0)) * green_ref[...]
    pltpu.make_async_copy(landed, landed, send_sem).wait()


def exchange(part, green):
    return pl.pallas_call(
        exchange_kernel,
        out_shape=jax.ShapeDtypeStruct((PARTS, KY), jnp.float32),
        in_specs=[pl.BlockSpec(memory_space=pltpu.VMEM)] * 2,
        out_specs=pl.BlockSpec(memory_space=pltpu.VMEM),
        scratch_shapes=[
            pltpu.VMEM(((DEVICES - 1) * PARTS, KY), jnp.float32),
            pltpu.SemaphoreType.DMA,
            pltpu.SemaphoreType.DMA,
        ],
        compiler_params=pltpu.CompilerParams(collective_id=0, has_side_effects=True),
    )(part, green)


def shards(cell_ids, masses, block_dest, block_count, screen):
    part = partial_modes(block_dest[:, 0], block_count, cell_ids, masses)
    z_freq = (position() - KZ // 2).astype(jnp.float32)
    y_freq = (lax.broadcasted_iota(jnp.int32, (1, KY), 1) - KY // 2).astype(jnp.float32)
    wave_sq = (2.0 * jnp.sin(math.pi * y_freq / NY)) ** 2 + (
        2.0 * jnp.sin(math.pi * z_freq / NZ)
    ) ** 2
    scr = screen[:, None]
    green = jnp.where((y_freq == 0.0) & (z_freq == 0.0), 0.0, -scr / (wave_sq + scr))
    green = green * (1.0 / math.sqrt(NY * NZ))
    modes = exchange(part, jnp.concatenate([green, green], axis=0))
    return jnp.moveaxis(modes.reshape(2, PL, KY), 0, 2)


def solution(mesh):
    return jax.shard_map(
        shards,
        mesh=mesh,
        in_specs=(
            P(("px", "py"), None),
            P(("px", "py"), None),
            P(("px", "py"), None),
            P(("px", "py")),
            P(),
        ),
        out_specs=P(None, None, ("px", "py")),
        check_vma=False,
    )
```

time: 739 us -> 61.7 us (0.08)
  the two profiles are of different devices: /device:TPU:0 before, /device:TPU:1 now
where the time goes in v2:
time: 61.7 us; the launch traced here: 61.2 us
  Pallas kernels  52.3 us (85%)
  local copies, waits for them, and re-layouts  8 us (13%)
  other arithmetic  0.74 us (1%)
    pallas_call x1, Pallas kernels, exchange(): pl.pallas_call(exchange_kernel, out_shape=jax.ShapeDtypeStruct((PARTS, KY...  27.6 us
    pallas_call x1, Pallas kernels, partial_modes(): pl.pallas_call(block_kernel, out_shape=jax.ShapeDtypeStruct((SLOTS * PART...  24.8 us
    unnamed x14, local copies, waits for them, and re-layouts  5.83 us
    reshape x1, local copies, waits for them, and re-layouts, shards(): return jnp.moveaxis(modes.reshape(2, PL, KY), 0, 2)  1.3 us

profile of v2, /device:TPU:1, one launch (start us, length us, event | category | flops | bytes accessed | tf_op | source)
XLA Modules:
  0.0 61.2 jit_solution(8787919923773037201)
XLA Ops:
  0.0 0.9 %broadcast_in_dim.19.count_ref = s32[1024,128]{1,0:T(8,128)S(1)} broadcast(s32[1024]{0:T(1024)} %param.10), dimensions={0} | broadcast | bytes 528384 | tf_op jit(solution)/shard_map/broadcast_in_dim | solution.py:169
  0.9 0.0 copy-start.1
  0.9 1.2 %copy-done.1 = bf16[2,2,512,256]{3,2,1,0:T(8,128)(2,1)S(1)} copy-done((bf16[2,2,512,256]{3,2,1,0:T(8,128)(2,1)S(1)}, bf16[2,2,512,256]{3,2,1,0:T(8,128)(2,1)}, u32[]{:S(2)}) %copy-start.1) | copy-done | bytes 1048600
  2.1 0.0 copy-start.2
  2.1 1.0 %copy-done.2 = s32[1024,128]{1,0:T(8,128)S(1)} copy-done((s32[1024,128]{1,0:T(8,128)S(1)}, s32[1024,128]{1,0:T(8,128)}, u32[]{:S(2)}) %copy-start.2) | copy-done | bytes 524312
  3.2 0.0 copy-start.3
  3.2 1.0 %copy-done.3 = bf16[288,512]{1,0:T(8,128)(2,1)S(1)} copy-done((bf16[288,512]{1,0:T(8,128)(2,1)S(1)}, bf16[288,512]{1,0:T(8,128)(2,1)}, u32[]{:S(2)}) %copy-start.3) | copy-done | bytes 294936
  4.1 0.0 copy-start.4
  4.1 0.9 %copy-done.4 = bf16[1024,128]{1,0:T(8,128)(2,1)S(1)} copy-done((bf16[1024,128]{1,0:T(8,128)(2,1)S(1)}, bf16[1024,128]{1,0:T(8,128)(2,1)}, u32[]{:S(2)}) %copy-start.4) | copy-done | bytes 262168
  5.1 0.0 copy-start.5
  5.1 0.7 %copy-done.5 = s32[1024,1]{0,1:T(1,128)S(1)} copy-done((s32[1024,1]{0,1:T(1,128)S(1)}, s32[1024,1]{0,1:T(1,128)}, u32[]{:S(2)}) %copy-start.5) | copy-done | bytes 4120
  5.8 0.0 copy-start.6
  5.8 24.8 %shard_map.73.part_ref = f32[2064,128]{1,0:T(8,128)S(1)} custom-call(s32[1024]{0:T(1024)S(1)} %bitcast.5, s32[1024,128]{1,0:T(8,128)S(1)} %broadcast_in_dim.19.count_ref, s32[1024,128]{1,0:T(8,128)S(1)} %copy-done.2, bf16[1024,128]{1,0:T(8,128)(2,1)S(1)} %copy-done.4, bf16[288,512]{1,0:T(8,128)(2,1)S(1)} %copy-done.3, bf16[2,2,512,256]{3,2,1,0:T(8,128)(2,1)S(1)} %copy-done.1), custom_call_target="tpu_custom_call" | custom-call | tf_op jit(solution)/shard_map/pallas_call | solution.py:170
  30.5 0.0 copy-start
  30.5 1.0 %copy-done = f32[2064,128]{1,0:T(8,128)} copy-done((f32[2064,128]{1,0:T(8,128)}, f32[2064,128]{1,0:T(8,128)S(1)}, u32[]{:S(2)}) %copy-start) | copy-done | bytes 1056792
  31.6 0.0 copy-done.6
  31.7 0.1 select_multiply_fusion
  31.8 0.6 pad_maximum_fusion.green_ref
  32.4 27.6 %shard_map.74 = f32[16,128]{1,0:T(8,128)} custom-call(f32[2064,128]{1,0:T(8,128)} %copy-done, f32[16,128]{1,0:T(8,128)} %pad_maximum_fusion.green_ref), custom_call_target="tpu_custom_call" | custom-call | tf_op jit(solution)/shard_map/pallas_call | solution.py:227
  59.9 1.3 %copy.10 = f32[2,8,128]{2,0,1:T(2,128)} copy(f32[2,8,128]{2,1,0:T(8,128)} %bitcast.6) | data formatting | bytes 16384 | tf_op jit(solution)/shard_map/reshape | solution.py:252
  (3 shorter events, 0.1 us)
Async XLA Ops:
  0.9 1.2 %copy-start.1 = (bf16[2,2,512,256]{3,2,1,0:T(8,128)(2,1)S(1)}, bf16[2,2,512,256]{3,2,1,0:T(8,128)(2,1)}, u32[]{:S(2)}) copy-start(bf16[2,2,512,256]{3,2,1,0:T(8,128)(2,1)} %constant.40.clone.y_ref) | copy-start | bytes 3145732
  2.1 1.0 %copy-start.2 = (s32[1024,128]{1,0:T(8,128)S(1)}, s32[1024,128]{1,0:T(8,128)}, u32[]{:S(2)}) copy-start(s32[1024,128]{1,0:T(8,128)} %cells_ref.1) | copy-start | bytes 1572868
  3.2 1.0 %copy-start.3 = (bf16[288,512]{1,0:T(8,128)(2,1)S(1)}, bf16[288,512]{1,0:T(8,128)(2,1)}, u32[]{:S(2)}) copy-start(bf16[288,512]{1,0:T(8,128)(2,1)} %constant.39.clone.z_ref) | copy-start | bytes 884740
  4.1 0.9 %copy-start.4 = (bf16[1024,128]{1,0:T(8,128)(2,1)S(1)}, bf16[1024,128]{1,0:T(8,128)(2,1)}, u32[]{:S(2)}) copy-start(bf16[1024,128]{1,0:T(8,128)(2,1)} %mass_ref.1) | copy-start | bytes 786436
  5.1 0.7 %copy-start.5 = (s32[1024,1]{0,1:T(1,128)S(1)}, s32[1024,1]{0,1:T(1,128)}, u32[]{:S(2)}) copy-start(s32[1024,1]{0,1:T(1,128)} %param.9) | copy-start | bytes 12292
  5.8 25.9 %copy-start.6 = (f32[8]{0:T(128)S(1)}, f32[8]{0:T(128)}, u32[]{:S(2)}) copy-start(f32[8]{0:T(128)} %param.11) | copy-start | bytes 100
  30.5 1.0 %copy-start = (f32[2064,128]{1,0:T(8,128)}, f32[2064,128]{1,0:T(8,128)S(1)}, u32[]{:S(2)}) copy-start(f32[2064,128]{1,0:T(8,128)S(1)} %shard_map.73.part_ref) | copy-start | bytes 3170308

commit v3 on v2

v3 whole, which is shorter than its diff:
```python
import math

import jax
import jax.numpy as jnp
import ml_dtypes
import numpy as np
from jax import lax
from jax.experimental import pallas as pl
from jax.experimental.pallas import tpu as pltpu
from jax.sharding import PartitionSpec as P

NY = 2048
NZ = 2048
PL = 8
KY = 128
KZ = 128
N_PX = 8
N_PY = 16
DEVICES = N_PX * N_PY
SUB = 128
Q = 32
UNROLL = 64
SPAN = N_PY * Q
HALF = 72
ROWS = 2 * HALF
HELD = PL // 2
PARTS = 2 * HELD

MESH = pl.DeviceIdType.MESH


def twiddle_factors(freqs, length):
    angle = 2.0 * np.pi * freqs / length
    nodes = (np.arange(512) + 0.5) * np.pi / 512
    waves = np.exp(-1j * (angle * SUB / 2)[:, None] * np.cos(nodes)[None, :])
    coefs = (2.0 / 512) * waves @ np.cos(nodes[:, None] * np.arange(Q)[None, :])
    coefs[:, 0] /= 2
    starts = np.arange(length // SUB) * SUB + (SUB - 1) / 2
    shift = np.exp(-1j * starts[:, None] * angle[None, :])
    return (shift[:, None, :] * coefs.T[None, :, :]).reshape(-1, len(freqs))


def two_parts(values):
    high = values.astype(ml_dtypes.bfloat16)
    low = (values - high.astype(np.float64)).astype(ml_dtypes.bfloat16)
    return high, low


def z_table():
    factors = twiddle_factors(np.arange(HALF) * (np.arange(HALF) <= 64), NZ)
    return np.concatenate(two_parts(np.concatenate([factors.real, factors.imag], axis=1).T))


def y_table():
    factors = twiddle_factors(np.arange(KY) - KY // 2, NY)
    real, imag = factors.real, factors.imag
    both = np.stack(
        [np.concatenate([real, imag], axis=1), np.concatenate([-imag, real], axis=1)]
    )
    return np.stack(two_parts(both))


def split(values):
    high = values.astype(jnp.bfloat16)
    return high, (values - high.astype(jnp.float32)).astype(jnp.bfloat16)


def dot(a, b):
    return jnp.dot(a, b, preferred_element_type=jnp.float32)


def tile_blocks(dest_ref, first_ref, second_ref):
    lane = lax.broadcasted_iota(jnp.int32, (PL, SUB), 1)
    plane = lax.broadcasted_iota(jnp.int32, (PL, SUB), 0)
    dest = [jnp.broadcast_to(dest_ref[r : r + 1, :], (PL, SUB)) for r in range(8)]

    def find(step, carry):
        first, second = carry
        for j in range(8):
            device = step * 8 + j
            tile = device * PL + plane
            most = total = jnp.zeros((PL, SUB), jnp.int32)
            for r in range(8):
                named = jnp.where(dest[r] == tile, lane + (SUB * r + 1), 0)
                most, total = jnp.maximum(most, named), total + named
            most = jnp.max(most, axis=1, keepdims=True)
            total = jnp.sum(total, axis=1, keepdims=True)
            first = jnp.where(lane == device, most, first)
            second = jnp.where(lane == device, jnp.minimum(total - most, PL * SUB), second)
        return first, second

    none = jnp.zeros((PL, SUB), jnp.int32)
    first_ref[...], second_ref[...] = lax.fori_loop(0, DEVICES // 8, find, (none, none))


def chain(ref, first, x):
    twice = x + x
    before, now = first, first * x
    ref[0:8, :] = before
    ref[8:16, :] = now
    for q in range(2, Q):
        before, now = now, twice * now - before
        ref[8 * q : 8 * q + 8, :] = now


def block_products(count_ref, cells_ref, mass_ref, blocks, chains):
    blocks[0] = jnp.zeros((Q, SUB), jnp.float32)
    lane = lax.broadcasted_iota(jnp.int32, (8, SUB), 1)
    number = lax.broadcasted_iota(jnp.int32, (8, SUB), 0)

    def step(group, carry):
        none = jnp.zeros((Q, SUB), jnp.bfloat16)
        first = pl.multiple_of(group * UNROLL, UNROLL)
        masses = mass_ref[pl.ds(first, UNROLL), :].astype(jnp.float32)
        counts = jnp.broadcast_to(count_ref[pl.ds(first // SUB, 1), :], (8, SUB))
        for eight in range(UNROLL // 8):
            z_chain, y_chain = chains[2 * eight], chains[2 * eight + 1]
            base = pl.multiple_of(first + 8 * eight, 8)
            cells = cells_ref[pl.ds(base, 8), :]
            count = jnp.take_along_axis(
                counts, number + lax.rem(base, SUB), axis=1, mode="promise_in_bounds"
            )
            weight = jnp.where(lane < count, masses[8 * eight : 8 * eight + 8], 0.0)
            z_at = ((cells & (SUB - 1)).astype(jnp.float32) - (SUB - 1) / 2) * (2 / SUB)
            y_at = (((cells >> 7) & (SUB - 1)).astype(jnp.float32) - (SUB - 1) / 2) * (2 / SUB)
            chain(z_chain, weight, z_at)
            chain(y_chain, jnp.ones_like(weight), y_at)
            lower_half = (cells >> 14).astype(jnp.float32)
            for pair in range(0, 8, 2):
                left, right = [], []
                for j in (pair, pair + 1):
                    rows = [pl.ds(64 * i + j, 8, stride=8) for i in range(Q // 8)]
                    left.append(split(jnp.concatenate([z_chain[r, :] for r in rows], axis=0)))
                    high, low = split(jnp.concatenate([y_chain[r, :] for r in rows], axis=0))
                    second = lower_half[j : j + 1]
                    first_half = (1.0 - second).astype(jnp.bfloat16)
                    second = second.astype(jnp.bfloat16)
                    right.append(
                        jnp.concatenate(
                            [high * first_half, high * second, low * first_half, low * second],
                            axis=0,
                        )
                    )
                left = jnp.concatenate(
                    [
                        jnp.concatenate([left[0][0], left[0][1], none, none], axis=0),
                        jnp.concatenate([none, none, left[1][0], left[1][1]], axis=0),
                    ],
                    axis=1,
                )
                part = lax.dot_general(
                    left,
                    jnp.concatenate(right, axis=1),
                    (((1,), (1,)), ((), ())),
                    preferred_element_type=jnp.float32,
                )
                for j in range(2):
                    blocks[base + (1 + pair + j)] = (
                        part[64 * j : 64 * j + 32] + part[64 * j + 32 : 64 * j + 64]
                    )
        return carry

    lax.fori_loop(0, cells_ref.shape[0] // UNROLL, step, 0)


def plane_modes(plane, first_ref, second_ref, blocks, tiles, half, z_ref, y_ref):
    upper = lax.broadcasted_iota(jnp.int32, (Q, SUB), 1) >= SUB // 2

    def named(device):
        return blocks[first_ref[plane, device]] + blocks[second_ref[plane, device]]

    def collect(step, carry):
        for j in range(4):
            col = step * 4 + j
            row = pl.multiple_of(col * Q, Q)
            for i in range(4):
                even = named(2 * i * N_PY + col)
                odd = named((2 * i + 1) * N_PY + col)
                tile = jnp.where(upper, odd, even)
                tile = tile + pltpu.roll(jnp.where(upper, even, odd), SUB // 2, 1)
                high, low = split(tile)
                tiles[pl.ds(row, Q), 256 * i : 256 * i + 128] = high
                tiles[pl.ds(row, Q), 256 * i + 128 : 256 * i + 256] = low
        return carry

    lax.fori_loop(0, N_PY // 4, collect, 0)
    for i in range(4):
        product = dot(z_ref[0:ROWS, :], tiles[:, 256 * i : 256 * i + 256])
        product = product[:, :SUB] + product[:, SUB:]
        product += dot(z_ref[ROWS:, :], tiles[:, 256 * i : 256 * i + 128])
        half[:, SUB * i : SUB * i + SUB] = product
    modes = []
    for c in range(2):
        high, low = split(half[HALF * c : HALF * c + HALF, :])
        modes.append(dot(high, y_ref[0, c]) + dot(low, y_ref[0, c]) + dot(high, y_ref[1, c]))
    plus, minus = modes[0] + modes[1], modes[0] - modes[1]
    last = jnp.broadcast_to(minus[64:65], (8, 2 * KY))
    top = lax.broadcasted_iota(jnp.int32, (8, 2 * KY), 0) == 0
    rows = jnp.concatenate([plus[:64], jnp.where(top, last, minus[:8]), minus[8:64]], axis=0)
    return [rows[:, :KY], rows[:, KY:]]


def slot_of(device):
    ahead = device // 64
    return ahead * (device - 64) + (1 - ahead) * (64 + lax.rem(128 - device, 64))


def mesh_kernel(
    dest_hbm, count_hbm, screen_ref, cells_hbm, mass_hbm, z_hbm, y_hbm, wave_hbm, out_ref,
    dest, count, cells, mass, z_ref, y_ref, wave, first, second, first_at, second_at,
    blocks, tiles, half, give, get, send, landed,
    load_sems, table_sems, give_sems, get_sems, send_sem, land_sem, *chains,
):
    px, py = lax.axis_index("px"), lax.axis_index("py")
    me = px * N_PY + py
    core = lax.rem(px, 2)
    sibling = px + 1 - 2 * core
    loads = [
        pltpu.make_async_copy(a, b, load_sems.at[i])
        for i, (a, b) in enumerate(
            [
                (dest_hbm, dest),
                (count_hbm, count),
                (cells_hbm, cells),
                (mass_hbm, mass),
                (z_hbm, z_ref),
                (y_hbm, y_ref),
                (wave_hbm.at[pl.ds(me, 1)], wave),
            ]
        )
    ]
    for load in loads:
        load.start()
    barrier = pltpu.get_barrier_semaphore()

    def greet(k, carry):
        to = lax.rem(me + k, DEVICES)
        pl.semaphore_signal(barrier, inc=1, device_id=(to // N_PY, to % N_PY), device_id_type=MESH)
        return carry

    lax.fori_loop(1, DEVICES, greet, 0)
    loads[0].wait()
    tile_blocks(dest, first, second)
    tables = [
        pltpu.make_async_copy(first, first_at, table_sems.at[0]),
        pltpu.make_async_copy(second, second_at, table_sems.at[1]),
    ]
    for table in tables:
        table.start()
    for load in loads[1:4]:
        load.wait()
    block_products(count, cells, mass, blocks, chains)
    for copy in loads[4:] + tables:
        copy.wait()
    pl.semaphore_wait(barrier, DEVICES - 1)

    def handover(j):
        rows = pl.ds(pl.multiple_of(j * 256, 256), 256)
        return pltpu.make_async_remote_copy(
            src_ref=give.at[rows],
            dst_ref=get.at[rows],
            send_sem=give_sems.at[j],
            recv_sem=get_sems.at[j],
            device_id=(sibling, py),
            device_id_type=MESH,
        )

    def other_plane(j, carry):
        plane = (1 - core) * HELD + j
        modes = plane_modes(plane, first_at, second_at, blocks, tiles, half, z_ref, y_ref)
        for c in range(2):
            give[pl.ds(pl.multiple_of(j * 256 + 128 * c, 128), 128), :] = modes[c]
        handover(j).start()
        return carry

    def own_plane(j, carry):
        plane = core * HELD + j
        modes = plane_modes(plane, first_at, second_at, blocks, tiles, half, z_ref, y_ref)
        handover(j).wait_recv()
        for c in range(2):
            added = modes[c] + get[pl.ds(pl.multiple_of(j * 256 + 128 * c, 128), 128), :]
            send[pl.ds(HELD * c + j, 128, stride=PARTS), :] = added
        return carry

    lax.fori_loop(0, HELD, other_plane, 0)
    lax.fori_loop(0, HELD, own_plane, 0)
    place = pl.multiple_of((core * 64 + (px // 2) * N_PY + py) * PARTS, PARTS)

    def post(k, carry):
        to = lax.rem(me + k, DEVICES)
        pltpu.make_async_remote_copy(
            src_ref=send.at[pl.ds(pl.multiple_of(slot_of(to) * PARTS, PARTS), PARTS)],
            dst_ref=landed.at[pl.ds(place, PARTS)],
            send_sem=send_sem,
            recv_sem=land_sem,
            device_id=(to // N_PY, to % N_PY),
            device_id_type=MESH,
        ).start()
        return carry

    lax.fori_loop(1, DEVICES, post, 0)
    landed[pl.ds(place, PARTS), :] = send[
        pl.ds(pl.multiple_of(slot_of(me) * PARTS, PARTS), PARTS), :
    ]
    bulk = landed.at[pl.ds(0, (DEVICES - 1) * PARTS)]
    pltpu.make_async_copy(bulk, bulk, land_sem).wait()
    for h in range(2):
        total = jnp.sum(landed[512 * h : 512 * h + 512, :].reshape(64, PARTS, KY), axis=0)
        for j in range(HELD):
            scr = screen_ref[HELD * h + j]
            wave_sq = wave[...]
            green = jnp.where(wave_sq == 0.0, 0.0, -scr / (wave_sq + scr))
            green = green * (1.0 / math.sqrt(NY * NZ))
            for c in range(2):
                row = total[HELD * c + j : HELD * c + j + 1, :]
                out_ref[HELD * h + j, c : c + 1, :] = row * green
    pltpu.make_async_copy(bulk, bulk, send_sem).wait()

    def sent(j, carry):
        handover(j).wait_send()
        return carry

    lax.fori_loop(0, HELD, sent, 0)


def wave_table():
    z_wave = (2.0 * np.sin(np.pi * (np.arange(KZ) - KZ // 2) / NZ)) ** 2
    y_wave = (2.0 * np.sin(np.pi * (np.arange(KY) - KY // 2) / NY)) ** 2
    return (z_wave[:, None] + y_wave[None, :]).astype(np.float32)


def shards(cell_ids, masses, block_dest, block_count, screen):
    blocks = cell_ids.shape[0]
    f32, bf16, i32 = jnp.float32, jnp.bfloat16, jnp.int32
    dma = pltpu.SemaphoreType.DMA
    modes = pl.pallas_call(
        mesh_kernel,
        out_shape=jax.ShapeDtypeStruct((PL, 2, KY), f32),
        in_specs=[
            pl.BlockSpec(memory_space=pltpu.SMEM if i == 2 else pl.ANY) for i in range(8)
        ],
        out_specs=pl.BlockSpec(memory_space=pltpu.VMEM),
        scratch_shapes=[
            pltpu.VMEM((8, SUB), i32),
            pltpu.VMEM((8, SUB), i32),
            pltpu.VMEM((blocks, SUB), i32),
            pltpu.VMEM((blocks, SUB), bf16),
            pltpu.VMEM((2 * ROWS, SPAN), bf16),
            pltpu.VMEM((2, 2, SPAN, 2 * KY), bf16),
            pltpu.VMEM((1, KY), f32),
            pltpu.VMEM((8, SUB), i32),
            pltpu.VMEM((8, SUB), i32),
            pltpu.SMEM((8, SUB), i32),
            pltpu.SMEM((8, SUB), i32),
            pltpu.VMEM((blocks + 1, Q, SUB), f32),
            pltpu.VMEM((SPAN, 8 * SUB), bf16),
            pltpu.VMEM((ROWS, SPAN), f32),
            pltpu.VMEM((HELD * 256, KY), f32),
            pltpu.VMEM((HELD * 256, KY), f32),
            pltpu.VMEM((DEVICES * PARTS, KY), f32),
            pltpu.VMEM((DEVICES * PARTS, KY), f32),
            dma((7,)),
            dma((2,)),
            dma((HELD,)),
            dma((HELD,)),
            dma,
            dma,
        ]
        + [pltpu.VMEM((Q * 8, SUB), f32)] * (UNROLL // 4),
        compiler_params=pltpu.CompilerParams(
            collective_id=0, has_side_effects=True, vmem_limit_bytes=48 << 20
        ),
    )(
        block_dest.reshape(8, SUB),
        block_count.reshape(8, SUB),
        screen,
        cell_ids,
        masses,
        jnp.asarray(z_table()),
        jnp.asarray(y_table()),
        jnp.asarray(wave_table()),
    )
    return jnp.swapaxes(modes, 1, 2)


def solution(mesh):
    return jax.shard_map(
        shards,
        mesh=mesh,
        in_specs=(
            P(("px", "py"), None),
            P(("px", "py"), None),
            P(("px", "py"), None),
            P(("px", "py")),
            P(),
        ),
        out_specs=P(None, None, ("px", "py")),
        check_vma=False,
    )
```

time: 61.7 us -> 57.2 us (0.927)
  Pallas kernels: 52.3 us -> 49.2 us
  other arithmetic: 0.74 us -> 0 us
    pallas_call x2 -> x1, Pallas kernels: 52.3 us -> 49.2 us  [shards(): pl.pallas_call(mesh_kernel, out_shape=jax.ShapeDtypeStruct((PL, 2, KY), f...]
    unnamed x14 -> x17, local copies, waits for them, and re-layouts: 5.83 us -> 7.64 us
    reshape x1 -> x0, local copies, waits for them, and re-layouts: 1.3 us -> none  [shards(): return jnp.moveaxis(modes.reshape(2, PL, KY), 0, 2)]
    broadcast_in_dim x1 -> x0, local copies, waits for them, and re-layouts: 0.87 us -> none  [partial_modes(): counts = jnp.broadcast_to(count[:, None], (blocks, SUB))]
where the time goes in v3:
time: 57.2 us; the launch traced here: 56.8 us
  Pallas kernels  49.2 us (86%)
  local copies, waits for them, and re-layouts  7.64 us (13%)
    pallas_call x1, Pallas kernels, shards(): pl.pallas_call(mesh_kernel, out_shape=jax.ShapeDtypeStruct((PL, 2, KY), f...  49.2 us
    unnamed x17, local copies, waits for them, and re-layouts  7.64 us

profile of v3, /device:TPU:1, one launch (start us, length us, event | category | flops | bytes accessed | tf_op | source)
XLA Modules:
  0.0 56.8 jit_solution(7030751559107195593)
XLA Ops:
  0.0 0.0 copy-start.7
  0.0 0.7 %copy-done.7 = f32[8]{0:T(128)S(1)} copy-done((f32[8]{0:T(128)S(1)}, f32[8]{0:T(128)}, u32[]{:S(2)}) %copy-start.7) | copy-done | bytes 56
  0.7 0.0 copy-start
  0.7 1.2 %copy-done = bf16[2,2,512,256]{3,2,1,0:T(8,128)(2,1)S(1)} copy-done((bf16[2,2,512,256]{3,2,1,0:T(8,128)(2,1)S(1)}, bf16[2,2,512,256]{3,2,1,0:T(8,128)(2,1)}, u32[]{:S(2)}) %copy-start) | copy-done | bytes 1048600
  1.9 0.0 copy-start.1
  1.9 1.0 %copy-done.1 = s32[1024,128]{1,0:T(8,128)S(1)} copy-done((s32[1024,128]{1,0:T(8,128)S(1)}, s32[1024,128]{1,0:T(8,128)}, u32[]{:S(2)}) %copy-start.1) | copy-done | bytes 524312
  2.9 0.0 copy-start.2
  2.9 1.0 %copy-done.2 = bf16[288,512]{1,0:T(8,128)(2,1)S(1)} copy-done((bf16[288,512]{1,0:T(8,128)(2,1)S(1)}, bf16[288,512]{1,0:T(8,128)(2,1)}, u32[]{:S(2)}) %copy-start.2) | copy-done | bytes 294936
  3.9 0.0 copy-start.3
  3.9 0.9 %copy-done.3 = bf16[1024,128]{1,0:T(8,128)(2,1)S(1)} copy-done((bf16[1024,128]{1,0:T(8,128)(2,1)S(1)}, bf16[1024,128]{1,0:T(8,128)(2,1)}, u32[]{:S(2)}) %copy-start.3) | copy-done | bytes 262168
  4.8 0.0 copy-start.4
  4.8 0.8 %copy-done.4 = f32[128,128]{1,0:T(8,128)S(1)} copy-done((f32[128,128]{1,0:T(8,128)S(1)}, f32[128,128]{1,0:T(8,128)}, u32[]{:S(2)}) %copy-start.4) | copy-done | bytes 65560
  5.7 0.0 copy-start.5
  5.7 0.7 %copy-done.5 = s32[1024,1]{0,1:T(1,128)S(1)} copy-done((s32[1024,1]{0,1:T(1,128)S(1)}, s32[1024,1]{0,1:T(1,128)}, u32[]{:S(2)}) %copy-start.5) | copy-done | bytes 4120
  6.4 0.0 copy-start.6
  6.4 0.7 %copy-done.6 = s32[1024]{0:T(1024)S(1)} copy-done((s32[1024]{0:T(1024)S(1)}, s32[1024]{0:T(1024)}, u32[]{:S(2)}) %copy-start.6) | copy-done | bytes 4120
  7.1 49.2 %shard_map.82 = f32[8,2,128]{2,1,0:T(2,128)S(1)} custom-call(s32[8,128]{1,0:T(8,128)S(1)} %bitcast.4, s32[8,128]{1,0:T(8,128)S(1)} %bitcast.5, f32[8]{0:T(128)S(1)} %copy-done.7, s32[1024,128]{1,0:T(8,128)S(1)} %copy-done.1, bf16[1024,128]{1,0:T(8,128)(2,1)S(1)} %copy-done.3, bf16[288,512]{1,0:T(8,128)(2,1)S(1)} %copy-done.2, ...), custom_call_target="tpu_custom_call" | custom-call | tf_op jit(solution)/shard_map/pallas_call | solution.py:336
  56.2 0.6 %copy.10 = f32[8,128,2]{1,2,0:T(2,128)} copy(f32[8,128,2]{1,2,0:T(2,128)S(1)} %bitcast.3) | data formatting | bytes 16384
Async XLA Ops:
  0.0 0.7 %copy-start.7 = (f32[8]{0:T(128)S(1)}, f32[8]{0:T(128)}, u32[]{:S(2)}) copy-start(f32[8]{0:T(128)} %screen_ref.1) | copy-start | bytes 100
  0.7 1.2 %copy-start = (bf16[2,2,512,256]{3,2,1,0:T(8,128)(2,1)S(1)}, bf16[2,2,512,256]{3,2,1,0:T(8,128)(2,1)}, u32[]{:S(2)}) copy-start(bf16[2,2,512,256]{3,2,1,0:T(8,128)(2,1)} %constant.7.clone.y_hbm) | copy-start | bytes 3145732
  1.9 1.0 %copy-start.1 = (s32[1024,128]{1,0:T(8,128)S(1)}, s32[1024,128]{1,0:T(8,128)}, u32[]{:S(2)}) copy-start(s32[1024,128]{1,0:T(8,128)} %cells_hbm.1) | copy-start | bytes 1572868
  2.9 1.0 %copy-start.2 = (bf16[288,512]{1,0:T(8,128)(2,1)S(1)}, bf16[288,512]{1,0:T(8,128)(2,1)}, u32[]{:S(2)}) copy-start(bf16[288,512]{1,0:T(8,128)(2,1)} %constant.6.clone.z_hbm) | copy-start | bytes 884740
  3.9 0.9 %copy-start.3 = (bf16[1024,128]{1,0:T(8,128)(2,1)S(1)}, bf16[1024,128]{1,0:T(8,128)(2,1)}, u32[]{:S(2)}) copy-start(bf16[1024,128]{1,0:T(8,128)(2,1)} %mass_hbm.1) | copy-start | bytes 786436
  4.8 0.8 %copy-start.4 = (f32[128,128]{1,0:T(8,128)S(1)}, f32[128,128]{1,0:T(8,128)}, u32[]{:S(2)}) copy-start(f32[128,128]{1,0:T(8,128)} %constant.8.clone.wave_hbm) | copy-start | bytes 196612
  5.7 0.7 %copy-start.5 = (s32[1024,1]{0,1:T(1,128)S(1)}, s32[1024,1]{0,1:T(1,128)}, u32[]{:S(2)}) copy-start(s32[1024,1]{0,1:T(1,128)} %param.10) | copy-start | bytes 12292
  6.4 0.7 %copy-start.6 = (s32[1024]{0:T(1024)S(1)}, s32[1024]{0:T(1024)}, u32[]{:S(2)}) copy-start(s32[1024]{0:T(1024)} %param.11) | copy-start | bytes 12292

commit v4 on v3

--- a/solution.py
+++ b/solution.py
@@ -21,8 +21,8 @@
 Q = 32
 UNROLL = 64
 SPAN = N_PY * Q
-HALF = 72
-ROWS = 2 * HALF
+ROWS = 144
+MEET = 80
 HELD = PL // 2
 PARTS = 2 * HELD
 
@@ -47,17 +47,18 @@
 
 
 def z_table():
-    factors = twiddle_factors(np.arange(HALF) * (np.arange(HALF) <= 64), NZ)
-    return np.concatenate(two_parts(np.concatenate([factors.real, factors.imag], axis=1).T))
+    factors = twiddle_factors(np.arange(65), NZ)
+    real, imag = factors.real.T, factors.imag.T
+    rows = [real[:64], imag[:64], real[64:], imag[64:], np.zeros((ROWS - 130, SPAN))]
+    return np.concatenate(two_parts(np.concatenate(rows)))
 
 
 def y_table():
     factors = twiddle_factors(np.arange(KY) - KY // 2, NY)
     real, imag = factors.real, factors.imag
-    both = np.stack(
-        [np.concatenate([real, imag], axis=1), np.concatenate([-imag, real], axis=1)]
-    )
-    return np.stack(two_parts(both))
+    both = [np.concatenate([real, imag], axis=1), np.concatenate([-imag, real], axis=1)]
+    parts = [two_parts(table) for table in both]
+    return np.stack([np.concatenate([high, high, low]) for high, low in parts])
 
 
 def split(values):
@@ -69,28 +70,23 @@
     return jnp.dot(a, b, preferred_element_type=jnp.float32)
 
 
-def tile_blocks(dest_ref, first_ref, second_ref):
+def tile_blocks(step, dest_ref, first_ref, second_ref):
     lane = lax.broadcasted_iota(jnp.int32, (PL, SUB), 1)
     plane = lax.broadcasted_iota(jnp.int32, (PL, SUB), 0)
-    dest = [jnp.broadcast_to(dest_ref[r : r + 1, :], (PL, SUB)) for r in range(8)]
-
-    def find(step, carry):
-        first, second = carry
-        for j in range(8):
-            device = step * 8 + j
-            tile = device * PL + plane
-            most = total = jnp.zeros((PL, SUB), jnp.int32)
-            for r in range(8):
-                named = jnp.where(dest[r] == tile, lane + (SUB * r + 1), 0)
-                most, total = jnp.maximum(most, named), total + named
-            most = jnp.max(most, axis=1, keepdims=True)
-            total = jnp.sum(total, axis=1, keepdims=True)
-            first = jnp.where(lane == device, most, first)
-            second = jnp.where(lane == device, jnp.minimum(total - most, PL * SUB), second)
-        return first, second
-
-    none = jnp.zeros((PL, SUB), jnp.int32)
-    first_ref[...], second_ref[...] = lax.fori_loop(0, DEVICES // 8, find, (none, none))
+    first, second = first_ref[...], second_ref[...]
+    for j in range(8):
+        device = step * 8 + j
+        tile = device * PL + plane
+        most = total = jnp.zeros((PL, SUB), jnp.int32)
+        for r in range(8):
+            dest = jnp.broadcast_to(dest_ref[r : r + 1, :], (PL, SUB))
+            named = jnp.where(dest == tile, lane + (SUB * r + 1), 0)
+            most, total = jnp.maximum(most, named), total + named
+        most = jnp.max(most, axis=1, keepdims=True)
+        total = jnp.sum(total, axis=1, keepdims=True)
+        first = jnp.where(lane == device, most, first)
+        second = jnp.where(lane == device, jnp.minimum(total - most, PL * SUB), second)
+    first_ref[...], second_ref[...] = first, second
 
 
 def chain(ref, first, x):
@@ -103,13 +99,14 @@
         ref[8 * q : 8 * q + 8, :] = now
 
 
-def block_products(count_ref, cells_ref, mass_ref, blocks, chains):
+def block_products(count_ref, cells_ref, mass_ref, blocks, chains, beside):
     blocks[0] = jnp.zeros((Q, SUB), jnp.float32)
     lane = lax.broadcasted_iota(jnp.int32, (8, SUB), 1)
     number = lax.broadcasted_iota(jnp.int32, (8, SUB), 0)
 
     def step(group, carry):
         none = jnp.zeros((Q, SUB), jnp.bfloat16)
+        beside(group)
         first = pl.multiple_of(group * UNROLL, UNROLL)
         masses = mass_ref[pl.ds(first, UNROLL), :].astype(jnp.float32)
         counts = jnp.broadcast_to(count_ref[pl.ds(first // SUB, 1), :], (8, SUB))
@@ -163,53 +160,59 @@
     lax.fori_loop(0, cells_ref.shape[0] // UNROLL, step, 0)
 
 
-def plane_modes(plane, first_ref, second_ref, blocks, tiles, half, z_ref, y_ref):
+def collect(plane, first_ref, second_ref, blocks, tiles):
     upper = lax.broadcasted_iota(jnp.int32, (Q, SUB), 1) >= SUB // 2
 
     def named(device):
         return blocks[first_ref[plane, device]] + blocks[second_ref[plane, device]]
 
-    def collect(step, carry):
-        for j in range(4):
-            col = step * 4 + j
-            row = pl.multiple_of(col * Q, Q)
-            for i in range(4):
-                even = named(2 * i * N_PY + col)
-                odd = named((2 * i + 1) * N_PY + col)
-                tile = jnp.where(upper, odd, even)
-                tile = tile + pltpu.roll(jnp.where(upper, even, odd), SUB // 2, 1)
-                high, low = split(tile)
-                tiles[pl.ds(row, Q), 256 * i : 256 * i + 128] = high
-                tiles[pl.ds(row, Q), 256 * i + 128 : 256 * i + 256] = low
-        return carry
-
-    lax.fori_loop(0, N_PY // 4, collect, 0)
-    for i in range(4):
-        product = dot(z_ref[0:ROWS, :], tiles[:, 256 * i : 256 * i + 256])
-        product = product[:, :SUB] + product[:, SUB:]
-        product += dot(z_ref[ROWS:, :], tiles[:, 256 * i : 256 * i + 128])
-        half[:, SUB * i : SUB * i + SUB] = product
-    modes = []
-    for c in range(2):
-        high, low = split(half[HALF * c : HALF * c + HALF, :])
-        modes.append(dot(high, y_ref[0, c]) + dot(low, y_ref[0, c]) + dot(high, y_ref[1, c]))
-    plus, minus = modes[0] + modes[1], modes[0] - modes[1]
-    last = jnp.broadcast_to(minus[64:65], (8, 2 * KY))
+    for col in range(N_PY):
+        for i in range(4):
+            even = named(2 * i * N_PY + col)
+            odd = named((2 * i + 1) * N_PY + col)
+            tile = jnp.where(upper, odd, even)
+            tile = tile + pltpu.roll(jnp.where(upper, even, odd), SUB // 2, 1)
+            for part, values in enumerate(split(tile)):
+                tiles[part, Q * col : Q * col + Q, SUB * i : SUB * i + SUB] = values
+
+
+def z_transform(j, tiles, half, z_ref):
+    for n in range(2):
+        lanes = slice(256 * n, 256 * n + 256)
+        product = dot(z_ref[...], tiles[0, :, lanes])
+        product = product[:ROWS] + product[ROWS:] + dot(z_ref[:ROWS, :], tiles[1, :, lanes])
+        high, low = split(product)
+        for c in range(2):
+            for place, part in enumerate((high, low, high)):
+                at = slice(SPAN * place + 256 * n, SPAN * place + 256 * n + 256)
+                half[c, MEET * j : MEET * j + 64, at] = part[64 * c : 64 * c + 64]
+                half[c, MEET * j + 64 : MEET * j + MEET, at] = part[128:ROWS]
+
+
+def y_transform(half, y_ref, stage):
+    real, imag = dot(half[0], y_ref[0]), dot(half[1], y_ref[1])
     top = lax.broadcasted_iota(jnp.int32, (8, 2 * KY), 0) == 0
-    rows = jnp.concatenate([plus[:64], jnp.where(top, last, minus[:8]), minus[8:64]], axis=0)
-    return [rows[:, :KY], rows[:, KY:]]
+    for j in range(HELD):
+        a, b = real[MEET * j : MEET * j + MEET], imag[MEET * j : MEET * j + MEET]
+        minus = a[:64] - b[:64]
+        last = jnp.broadcast_to(a[64:65] - b[65:66], (8, 2 * KY))
+        minus = jnp.concatenate([jnp.where(top, last, minus[:8]), minus[8:]], axis=0)
+        for c in range(2):
+            lanes = slice(KY * c, KY * c + KY)
+            stage[j, c, 0:64, :] = (a[:64] + b[:64])[:, lanes]
+            stage[j, c, 64:128, :] = minus[:, lanes]
 
 
 def slot_of(device):
-    ahead = device // 64
-    return ahead * (device - 64) + (1 - ahead) * (64 + lax.rem(128 - device, 64))
+    ahead = device >> 6
+    return ahead * (device - 64) + (1 - ahead) * (64 + ((128 - device) & 63))
 
 
 def mesh_kernel(
     dest_hbm, count_hbm, screen_ref, cells_hbm, mass_hbm, z_hbm, y_hbm, wave_hbm, out_ref,
     dest, count, cells, mass, z_ref, y_ref, wave, first, second, first_at, second_at,
-    blocks, tiles, half, give, get, send, landed,
-    load_sems, table_sems, give_sems, get_sems, send_sem, land_sem, *chains,
+    blocks, tiles_a, tiles_b, half, stage, get, send, landed,
+    load_sems, table_sems, give_sem, get_sem, send_sem, land_sem, *chains,
 ):
     px, py = lax.axis_index("px"), lax.axis_index("py")
     me = px * N_PY + py
@@ -233,67 +236,74 @@
         load.start()
     barrier = pltpu.get_barrier_semaphore()
 
-    def greet(k, carry):
-        to = lax.rem(me + k, DEVICES)
-        pl.semaphore_signal(barrier, inc=1, device_id=(to // N_PY, to % N_PY), device_id_type=MESH)
-        return carry
-
-    lax.fori_loop(1, DEVICES, greet, 0)
-    loads[0].wait()
-    tile_blocks(dest, first, second)
+    def greet(k):
+        to = (me + k) & (DEVICES - 1)
+        pl.semaphore_signal(
+            barrier, inc=1, device_id=(to >> 4, to & (N_PY - 1)), device_id_type=MESH
+        )
+
+    for k in range(1, 16):
+        greet(k)
+    first[...] = jnp.zeros_like(first)
+    second[...] = jnp.zeros_like(second)
+
+    def beside(group):
+        for j in range(7):
+            greet(16 + group * 7 + j)
+        tile_blocks(group, dest, first, second)
+
+    for load in loads[:4]:
+        load.wait()
+    block_products(count, cells, mass, blocks, chains, beside)
     tables = [
         pltpu.make_async_copy(first, first_at, table_sems.at[0]),
         pltpu.make_async_copy(second, second_at, table_sems.at[1]),
     ]
     for table in tables:
         table.start()
-    for load in loads[1:4]:
-        load.wait()
-    block_products(count, cells, mass, blocks, chains)
     for copy in loads[4:] + tables:
         copy.wait()
-    pl.semaphore_wait(barrier, DEVICES - 1)
-
-    def handover(j):
-        rows = pl.ds(pl.multiple_of(j * 256, 256), 256)
-        return pltpu.make_async_remote_copy(
-            src_ref=give.at[rows],
-            dst_ref=get.at[rows],
-            send_sem=give_sems.at[j],
-            recv_sem=get_sems.at[j],
-            device_id=(sibling, py),
-            device_id_type=MESH,
-        )
-
-    def other_plane(j, carry):
-        plane = (1 - core) * HELD + j
-        modes = plane_modes(plane, first_at, second_at, blocks, tiles, half, z_ref, y_ref)
+    handover = pltpu.make_async_remote_copy(
+        src_ref=stage.at[0],
+        dst_ref=get,
+        send_sem=give_sem,
+        recv_sem=get_sem,
+        device_id=(sibling, py),
+        device_id_type=MESH,
+    )
+
+    def batch(b, carry):
+        base = HELD * (b * core + (1 - b) * (1 - core))
+        tiles = (tiles_a, tiles_b)
+        collect(base, first_at, second_at, blocks, tiles[0])
+        for j in range(HELD):
+            z_transform(j, tiles[j % 2], half, z_ref)
+            if j + 1 < HELD:
+                collect(base + (j + 1), first_at, second_at, blocks, tiles[(j + 1) % 2])
+        y_transform(half, y_ref, stage.at[b])
+
+        @pl.when(b == 0)
+        def _():
+            pl.semaphore_wait(barrier, DEVICES - 1)
+            handover.start()
+
+        return carry
+
+    lax.fori_loop(0, 2, batch, 0)
+    handover.wait_recv()
+    for j in range(HELD):
         for c in range(2):
-            give[pl.ds(pl.multiple_of(j * 256 + 128 * c, 128), 128), :] = modes[c]
-        handover(j).start()
-        return carry
-
-    def own_plane(j, carry):
-        plane = core * HELD + j
-        modes = plane_modes(plane, first_at, second_at, blocks, tiles, half, z_ref, y_ref)
-        handover(j).wait_recv()
-        for c in range(2):
-            added = modes[c] + get[pl.ds(pl.multiple_of(j * 256 + 128 * c, 128), 128), :]
-            send[pl.ds(HELD * c + j, 128, stride=PARTS), :] = added
-        return carry
-
-    lax.fori_loop(0, HELD, other_plane, 0)
-    lax.fori_loop(0, HELD, own_plane, 0)
+            send[pl.ds(HELD * c + j, 128, stride=PARTS), :] = stage[1, j, c] + get[j, c]
     place = pl.multiple_of((core * 64 + (px // 2) * N_PY + py) * PARTS, PARTS)
 
     def post(k, carry):
-        to = lax.rem(me + k, DEVICES)
+        to = (me + k) & (DEVICES - 1)
         pltpu.make_async_remote_copy(
             src_ref=send.at[pl.ds(pl.multiple_of(slot_of(to) * PARTS, PARTS), PARTS)],
             dst_ref=landed.at[pl.ds(place, PARTS)],
             send_sem=send_sem,
             recv_sem=land_sem,
-            device_id=(to // N_PY, to % N_PY),
+            device_id=(to >> 4, to & (N_PY - 1)),
             device_id_type=MESH,
         ).start()
         return carry
@@ -315,12 +325,7 @@
                 row = total[HELD * c + j : HELD * c + j + 1, :]
                 out_ref[HELD * h + j, c : c + 1, :] = row * green
     pltpu.make_async_copy(bulk, bulk, send_sem).wait()
-
-    def sent(j, carry):
-        handover(j).wait_send()
-        return carry
-
-    lax.fori_loop(0, HELD, sent, 0)
+    handover.wait_send()
 
 
 def wave_table():
@@ -346,29 +351,30 @@
             pltpu.VMEM((blocks, SUB), i32),
             pltpu.VMEM((blocks, SUB), bf16),
             pltpu.VMEM((2 * ROWS, SPAN), bf16),
-            pltpu.VMEM((2, 2, SPAN, 2 * KY), bf16),
+            pltpu.VMEM((2, 3 * SPAN, 2 * KY), bf16),
             pltpu.VMEM((1, KY), f32),
             pltpu.VMEM((8, SUB), i32),
             pltpu.VMEM((8, SUB), i32),
             pltpu.SMEM((8, SUB), i32),
             pltpu.SMEM((8, SUB), i32),
             pltpu.VMEM((blocks + 1, Q, SUB), f32),
-            pltpu.VMEM((SPAN, 8 * SUB), bf16),
-            pltpu.VMEM((ROWS, SPAN), f32),
-            pltpu.VMEM((HELD * 256, KY), f32),
-            pltpu.VMEM((HELD * 256, KY), f32),
+            pltpu.VMEM((2, SPAN, SPAN), bf16),
+            pltpu.VMEM((2, SPAN, SPAN), bf16),
+            pltpu.VMEM((2, HELD * MEET, 3 * SPAN), bf16),
+            pltpu.VMEM((2, HELD, 2, KZ, KY), f32),
+            pltpu.VMEM((HELD, 2, KZ, KY), f32),
             pltpu.VMEM((DEVICES * PARTS, KY), f32),
             pltpu.VMEM((DEVICES * PARTS, KY), f32),
             dma((7,)),
             dma((2,)),
-            dma((HELD,)),
-            dma((HELD,)),
+            dma,
+            dma,
             dma,
             dma,
         ]
         + [pltpu.VMEM((Q * 8, SUB), f32)] * (UNROLL // 4),
         compiler_params=pltpu.CompilerParams(
-            collective_id=0, has_side_effects=True, vmem_limit_bytes=48 << 20
+            collective_id=0, has_side_effects=True, vmem_limit_bytes=60 << 20
         ),
     )(
         block_dest.reshape(8, SUB),

time: 57.2 us -> 42.8 us (0.75)
  Pallas kernels: 49.2 us -> 41.3 us
  local copies, waits for them, and re-layouts: 7.64 us -> 1.3 us
    pallas_call x1, Pallas kernels: 49.2 us -> 41.3 us  [shards(): pl.pallas_call(mesh_kernel, out_shape=jax.ShapeDtypeStruct((PL, 2, KY), f...]
    unnamed x17 -> x1, local copies, waits for them, and re-layouts: 7.64 us -> 1.3 us
where the time goes in v4:
time: 42.8 us; the launch traced here: 42.6 us
  Pallas kernels  41.3 us (96%)
  local copies, waits for them, and re-layouts  1.3 us (3%)
    pallas_call x1, Pallas kernels, shards(): pl.pallas_call(mesh_kernel, out_shape=jax.ShapeDtypeStruct((PL, 2, KY), f...  41.3 us
    unnamed x1, local copies, waits for them, and re-layouts  1.3 us

profile of v4, /device:TPU:1, one launch (start us, length us, event | category | flops | bytes accessed | tf_op | source)
XLA Modules:
  0.0 42.6 jit_solution(12218976080289959180)
XLA Ops:
  0.0 41.3 %shard_map.82 = f32[8,2,128]{2,1,0:T(2,128)} custom-call(s32[8,128]{1,0:T(8,128)} %bitcast.4, s32[8,128]{1,0:T(8,128)} %bitcast.5, f32[8]{0:T(128)} %screen_ref.1, s32[1024,128]{1,0:T(8,128)} %cells_hbm.1, bf16[1024,128]{1,0:T(8,128)(2,1)} %mass_hbm.1, bf16[288,512]{1,0:T(8,128)(2,1)} %constant.6.clone.z_hbm, bf16[2,1536,256]{2,1,0:T(8,128)(2,1)} %constant.7.clone.y_hbm, ...), custom_call_target="tpu_custom_call" | custom-call | tf_op jit(solution)/shard_map/pallas_call | solution.py:341
  41.3 1.3 %copy.10 = f32[8,128,2]{1,2,0:T(2,128)} copy(f32[8,128,2]{1,2,0:T(2,128)} %bitcast.3) | data formatting | bytes 16384

commit v5 on v4

--- a/solution.py
+++ b/solution.py
@@ -19,7 +19,7 @@
 DEVICES = N_PX * N_PY
 SUB = 128
 Q = 32
-UNROLL = 64
+UNROLL = 128
 SPAN = N_PY * Q
 ROWS = 144
 MEET = 80
@@ -99,14 +99,17 @@
         ref[8 * q : 8 * q + 8, :] = now
 
 
-def block_products(count_ref, cells_ref, mass_ref, blocks, chains, beside):
+def block_products(count_ref, cells_ref, mass_ref, blocks, chains, beside, between):
     blocks[0] = jnp.zeros((Q, SUB), jnp.float32)
     lane = lax.broadcasted_iota(jnp.int32, (8, SUB), 1)
     number = lax.broadcasted_iota(jnp.int32, (8, SUB), 0)
 
+    def both(group, carry):
+        beside(group)
+        return step(group, carry)
+
     def step(group, carry):
         none = jnp.zeros((Q, SUB), jnp.bfloat16)
-        beside(group)
         first = pl.multiple_of(group * UNROLL, UNROLL)
         masses = mass_ref[pl.ds(first, UNROLL), :].astype(jnp.float32)
         counts = jnp.broadcast_to(count_ref[pl.ds(first // SUB, 1), :], (8, SUB))
@@ -157,7 +160,10 @@
                     )
         return carry
 
-    lax.fori_loop(0, cells_ref.shape[0] // UNROLL, step, 0)
+    steps = cells_ref.shape[0] // UNROLL
+    lax.fori_loop(0, steps // 2, both, 0)
+    between()
+    lax.fori_loop(steps // 2, steps, step, 0)
 
 
 def collect(plane, first_ref, second_ref, blocks, tiles):
@@ -242,25 +248,32 @@
             barrier, inc=1, device_id=(to >> 4, to & (N_PY - 1)), device_id_type=MESH
         )
 
-    for k in range(1, 16):
+    def greet_some(k, carry):
         greet(k)
+        return carry
+
+    lax.fori_loop(1, 64, greet_some, 0)
     first[...] = jnp.zeros_like(first)
     second[...] = jnp.zeros_like(second)
 
     def beside(group):
-        for j in range(7):
-            greet(16 + group * 7 + j)
-        tile_blocks(group, dest, first, second)
+        for j in range(16):
+            greet(64 + group * 16 + j)
+        for j in range(4):
+            tile_blocks(group * 4 + j, dest, first, second)
 
     for load in loads[:4]:
         load.wait()
-    block_products(count, cells, mass, blocks, chains, beside)
     tables = [
         pltpu.make_async_copy(first, first_at, table_sems.at[0]),
         pltpu.make_async_copy(second, second_at, table_sems.at[1]),
     ]
-    for table in tables:
-        table.start()
+
+    def between():
+        for table in tables:
+            table.start()
+
+    block_products(count, cells, mass, blocks, chains, beside, between)
     for copy in loads[4:] + tables:
         copy.wait()
     handover = pltpu.make_async_remote_copy(

time: 42.8 us -> 40.3 us (0.942)
  Pallas kernels: 41.3 us -> 38.8 us
    pallas_call x1, Pallas kernels: 41.3 us -> 38.8 us  [shards(): pl.pallas_call(mesh_kernel, out_shape=jax.ShapeDtypeStruct((PL, 2, KY), f...]
where the time goes in v5:
time: 40.3 us; the launch traced here: 40.1 us
  Pallas kernels  38.8 us (96%)
  local copies, waits for them, and re-layouts  1.3 us (3%)
    pallas_call x1, Pallas kernels, shards(): pl.pallas_call(mesh_kernel, out_shape=jax.ShapeDtypeStruct((PL, 2, KY), f...  38.8 us
    unnamed x1, local copies, waits for them, and re-layouts  1.3 us

profile of v5, /device:TPU:1, one launch (start us, length us, event | category | flops | bytes accessed | tf_op | source)
XLA Modules:
  0.0 40.1 jit_solution(16832295767345643264)
XLA Ops:
  0.0 38.8 %shard_map.82 = f32[8,2,128]{2,1,0:T(2,128)} custom-call(s32[8,128]{1,0:T(8,128)} %bitcast.4, s32[8,128]{1,0:T(8,128)} %bitcast.5, f32[8]{0:T(128)} %screen_ref.1, s32[1024,128]{1,0:T(8,128)} %cells_hbm.1, bf16[1024,128]{1,0:T(8,128)(2,1)} %mass_hbm.1, bf16[288,512]{1,0:T(8,128)(2,1)} %constant.6.clone.z_hbm, bf16[2,1536,256]{2,1,0:T(8,128)(2,1)} %constant.7.clone.y_hbm, ...), custom_call_target="tpu_custom_call" | custom-call | tf_op jit(solution)/shard_map/pallas_call | solution.py:354
  38.8 1.3 %copy.10 = f32[8,128,2]{1,2,0:T(2,128)} copy(f32[8,128,2]{1,2,0:T(2,128)} %bitcast.3) | data formatting | bytes 16384

commit v6 on v5

--- a/solution.py
+++ b/solution.py
@@ -70,23 +70,46 @@
     return jnp.dot(a, b, preferred_element_type=jnp.float32)
 
 
-def tile_blocks(step, dest_ref, first_ref, second_ref):
+def merge(a, b, shift, better):
+    high = (lax.broadcasted_iota(jnp.int32, (PL, SUB), 1) & shift) != 0
+    swapped = jnp.where(high, a, b)
+    other = pltpu.roll(swapped, SUB - shift, 1)
+    if 2 * shift < SUB:
+        other = jnp.where(high, pltpu.roll(swapped, shift, 1), other)
+    return better(jnp.where(high, b, a), other)
+
+
+def merge_all(values, shift, better):
+    while len(values) > 1:
+        half = len(values) // 2
+        values = [merge(values[n], values[n + half], shift, better) for n in range(half)]
+        shift //= 2
+    return values[0]
+
+
+def tile_blocks(step, dest_ref, most_ref, least_ref):
     lane = lax.broadcasted_iota(jnp.int32, (PL, SUB), 1)
     plane = lax.broadcasted_iota(jnp.int32, (PL, SUB), 0)
-    first, second = first_ref[...], second_ref[...]
+    names = [lane + (SUB * r + 1) for r in range(8)]
+    dest = [jnp.broadcast_to(dest_ref[r : r + 1, :], (PL, SUB)) - plane for r in range(8)]
+    mosts, leasts = [], []
     for j in range(8):
-        device = step * 8 + j
-        tile = device * PL + plane
-        most = total = jnp.zeros((PL, SUB), jnp.int32)
+        named = [dest[r] == (step + 16 * j) * PL for r in range(8)]
+        most, least = jnp.zeros((PL, SUB), jnp.int32), jnp.full((PL, SUB), 2 * PL * SUB, jnp.int32)
         for r in range(8):
-            dest = jnp.broadcast_to(dest_ref[r : r + 1, :], (PL, SUB))
-            named = jnp.where(dest == tile, lane + (SUB * r + 1), 0)
-            most, total = jnp.maximum(most, named), total + named
-        most = jnp.max(most, axis=1, keepdims=True)
-        total = jnp.sum(total, axis=1, keepdims=True)
-        first = jnp.where(lane == device, most, first)
-        second = jnp.where(lane == device, jnp.minimum(total - most, PL * SUB), second)
-    first_ref[...], second_ref[...] = first, second
+            most = jnp.where(named[r], names[r], most)
+            least = jnp.where(named[7 - r], names[7 - r], least)
+        mosts.append(most)
+        leasts.append(least)
+    most_ref[step] = merge_all(mosts, 64, jnp.maximum)
+    least_ref[step] = merge_all(leasts, 64, jnp.minimum)
+
+
+def tile_table(most_ref, least_ref, first_ref, second_ref):
+    most = merge_all([most_ref[n] for n in range(16)], 8, jnp.maximum)
+    least = merge_all([least_ref[n] for n in range(16)], 8, jnp.minimum)
+    first_ref[...] = most
+    second_ref[...] = jnp.where(least < most, least, 0)
 
 
 def chain(ref, first, x):
@@ -178,25 +201,29 @@
             odd = named((2 * i + 1) * N_PY + col)
             tile = jnp.where(upper, odd, even)
             tile = tile + pltpu.roll(jnp.where(upper, even, odd), SUB // 2, 1)
-            for part, values in enumerate(split(tile)):
-                tiles[part, Q * col : Q * col + Q, SUB * i : SUB * i + SUB] = values
+            tiles[Q * col : Q * col + Q, SUB * i : SUB * i + SUB] = tile
 
 
 def z_transform(j, tiles, half, z_ref):
     for n in range(2):
         lanes = slice(256 * n, 256 * n + 256)
-        product = dot(z_ref[...], tiles[0, :, lanes])
-        product = product[:ROWS] + product[ROWS:] + dot(z_ref[:ROWS, :], tiles[1, :, lanes])
-        high, low = split(product)
+        product = 0.0
+        for k in range(2):
+            depth = slice(256 * k, 256 * k + 256)
+            high, low = split(tiles[depth, lanes])
+            both = dot(z_ref[:, depth], high)
+            product += both[:ROWS] + both[ROWS:] + dot(z_ref[:ROWS, depth], low)
         for c in range(2):
-            for place, part in enumerate((high, low, high)):
-                at = slice(SPAN * place + 256 * n, SPAN * place + 256 * n + 256)
-                half[c, MEET * j : MEET * j + 64, at] = part[64 * c : 64 * c + 64]
-                half[c, MEET * j + 64 : MEET * j + MEET, at] = part[128:ROWS]
+            half[c, MEET * j : MEET * j + 64, lanes] = product[64 * c : 64 * c + 64]
+            half[c, MEET * j + 64 : MEET * j + MEET, lanes] = product[128:ROWS]
 
 
 def y_transform(half, y_ref, stage):
-    real, imag = dot(half[0], y_ref[0]), dot(half[1], y_ref[1])
+    sides = []
+    for c in range(2):
+        high, low = split(half[c])
+        sides.append(dot(jnp.concatenate([high, low, high], axis=1), y_ref[c]))
+    real, imag = sides
     top = lax.broadcasted_iota(jnp.int32, (8, 2 * KY), 0) == 0
     for j in range(HELD):
         a, b = real[MEET * j : MEET * j + MEET], imag[MEET * j : MEET * j + MEET]
@@ -216,7 +243,7 @@
 
 def mesh_kernel(
     dest_hbm, count_hbm, screen_ref, cells_hbm, mass_hbm, z_hbm, y_hbm, wave_hbm, out_ref,
-    dest, count, cells, mass, z_ref, y_ref, wave, first, second, first_at, second_at,
+    dest, count, cells, mass, z_ref, y_ref, wave, most, least, first, second, first_at, second_at,
     blocks, tiles_a, tiles_b, half, stage, get, send, landed,
     load_sems, table_sems, give_sem, get_sem, send_sem, land_sem, *chains,
 ):
@@ -238,7 +265,7 @@
             ]
         )
     ]
-    for load in loads:
+    for load in loads[:4]:
         load.start()
     barrier = pltpu.get_barrier_semaphore()
 
@@ -248,19 +275,19 @@
             barrier, inc=1, device_id=(to >> 4, to & (N_PY - 1)), device_id_type=MESH
         )
 
-    def greet_some(k, carry):
+    def greet_some(step, carry):
+        for j in range(8):
+            greet(7 + 8 * step + j)
+        return carry
+
+    for k in range(1, 7):
         greet(k)
-        return carry
-
-    lax.fori_loop(1, 64, greet_some, 0)
-    first[...] = jnp.zeros_like(first)
-    second[...] = jnp.zeros_like(second)
+    lax.fori_loop(0, 15, greet_some, 0)
+    greet(DEVICES - 1)
 
     def beside(group):
-        for j in range(16):
-            greet(64 + group * 16 + j)
         for j in range(4):
-            tile_blocks(group * 4 + j, dest, first, second)
+            tile_blocks(group * 4 + j, dest, most, least)
 
     for load in loads[:4]:
         load.wait()
@@ -270,8 +297,9 @@
     ]
 
     def between():
-        for table in tables:
-            table.start()
+        tile_table(most, least, first, second)
+        for copy in tables + loads[4:]:
+            copy.start()
 
     block_products(count, cells, mass, blocks, chains, beside, between)
     for copy in loads[4:] + tables:
@@ -366,14 +394,16 @@
             pltpu.VMEM((2 * ROWS, SPAN), bf16),
             pltpu.VMEM((2, 3 * SPAN, 2 * KY), bf16),
             pltpu.VMEM((1, KY), f32),
+            pltpu.VMEM((16, PL, SUB), i32),
+            pltpu.VMEM((16, PL, SUB), i32),
             pltpu.VMEM((8, SUB), i32),
             pltpu.VMEM((8, SUB), i32),
             pltpu.SMEM((8, SUB), i32),
             pltpu.SMEM((8, SUB), i32),
             pltpu.VMEM((blocks + 1, Q, SUB), f32),
-            pltpu.VMEM((2, SPAN, SPAN), bf16),
-            pltpu.VMEM((2, SPAN, SPAN), bf16),
-            pltpu.VMEM((2, HELD * MEET, 3 * SPAN), bf16),
+            pltpu.VMEM((SPAN, SPAN), f32),
+            pltpu.VMEM((SPAN, SPAN), f32),
+            pltpu.VMEM((2, HELD * MEET, SPAN), f32),
             pltpu.VMEM((2, HELD, 2, KZ, KY), f32),
             pltpu.VMEM((HELD, 2, KZ, KY), f32),
             pltpu.VMEM((DEVICES * PARTS, KY), f32),

time: 40.3 us -> 39.7 us (0.985)
  Pallas kernels: 38.8 us -> 38.3 us
    pallas_call x1, Pallas kernels: 38.8 us -> 38.3 us  [shards(): pl.pallas_call(mesh_kernel, out_shape=jax.ShapeDtypeStruct((PL, 2, KY), f...]
where the time goes in v6:
time: 39.7 us; the launch traced here: 39.6 us
  Pallas kernels  38.3 us (96%)
  local copies, waits for them, and re-layouts  1.3 us (3%)
    pallas_call x1, Pallas kernels, shards(): pl.pallas_call(mesh_kernel, out_shape=jax.ShapeDtypeStruct((PL, 2, KY), f...  38.3 us
    unnamed x1, local copies, waits for them, and re-layouts  1.3 us

profile of v6, /device:TPU:1, one launch (start us, length us, event | category | flops | bytes accessed | tf_op | source)
XLA Modules:
  0.0 39.6 jit_solution(6785429002771300139)
XLA Ops:
  0.0 38.3 %shard_map.82 = f32[8,2,128]{2,1,0:T(2,128)} custom-call(s32[8,128]{1,0:T(8,128)} %bitcast.4, s32[8,128]{1,0:T(8,128)} %bitcast.5, f32[8]{0:T(128)} %screen_ref.1, s32[1024,128]{1,0:T(8,128)} %cells_hbm.1, bf16[1024,128]{1,0:T(8,128)(2,1)} %mass_hbm.1, bf16[288,512]{1,0:T(8,128)(2,1)} %constant.6.clone.z_hbm, bf16[2,1536,256]{2,1,0:T(8,128)(2,1)} %constant.7.clone.y_hbm, ...), custom_call_target="tpu_custom_call" | custom-call | tf_op jit(solution)/shard_map/pallas_call | solution.py:382
  38.3 1.3 %copy.10 = f32[8,128,2]{1,2,0:T(2,128)} copy(f32[8,128,2]{1,2,0:T(2,128)} %bitcast.3) | data formatting | bytes 16384

commit v7 on v6

--- a/solution.py
+++ b/solution.py
@@ -19,7 +19,7 @@
 DEVICES = N_PX * N_PY
 SUB = 128
 Q = 32
-UNROLL = 128
+UNROLL = 256
 SPAN = N_PY * Q
 ROWS = 144
 MEET = 80
@@ -135,13 +135,19 @@
         none = jnp.zeros((Q, SUB), jnp.bfloat16)
         first = pl.multiple_of(group * UNROLL, UNROLL)
         masses = mass_ref[pl.ds(first, UNROLL), :].astype(jnp.float32)
-        counts = jnp.broadcast_to(count_ref[pl.ds(first // SUB, 1), :], (8, SUB))
+        counts = [
+            jnp.broadcast_to(count_ref[pl.ds(first // SUB + h, 1), :], (8, SUB))
+            for h in range(UNROLL // SUB)
+        ]
         for eight in range(UNROLL // 8):
             z_chain, y_chain = chains[2 * eight], chains[2 * eight + 1]
             base = pl.multiple_of(first + 8 * eight, 8)
             cells = cells_ref[pl.ds(base, 8), :]
             count = jnp.take_along_axis(
-                counts, number + lax.rem(base, SUB), axis=1, mode="promise_in_bounds"
+                counts[8 * eight // SUB],
+                number + 8 * eight % SUB,
+                axis=1,
+                mode="promise_in_bounds",
             )
             weight = jnp.where(lane < count, masses[8 * eight : 8 * eight + 8], 0.0)
             z_at = ((cells & (SUB - 1)).astype(jnp.float32) - (SUB - 1) / 2) * (2 / SUB)
@@ -286,8 +292,8 @@
     greet(DEVICES - 1)
 
     def beside(group):
-        for j in range(4):
-            tile_blocks(group * 4 + j, dest, most, least)
+        for j in range(8):
+            tile_blocks(group * 8 + j, dest, most, least)
 
     for load in loads[:4]:
         load.wait()

time: 39.7 us -> 38.9 us (0.980)
  Pallas kernels: 38.3 us -> 37.4 us
    pallas_call x1, Pallas kernels: 38.3 us -> 37.4 us  [shards(): pl.pallas_call(mesh_kernel, out_shape=jax.ShapeDtypeStruct((PL, 2, KY), f...]
where the time goes in v7:
time: 38.9 us; the launch traced here: 38.7 us
  Pallas kernels  37.4 us (96%)
  local copies, waits for them, and re-layouts  1.3 us (3%)
    pallas_call x1, Pallas kernels, shards(): pl.pallas_call(mesh_kernel, out_shape=jax.ShapeDtypeStruct((PL, 2, KY), f...  37.4 us
    unnamed x1, local copies, waits for them, and re-layouts  1.3 us

profile of v7, /device:TPU:1, one launch (start us, length us, event | category | flops | bytes accessed | tf_op | source)
XLA Modules:
  0.0 38.7 jit_solution(18399232838668735985)
XLA Ops:
  0.0 37.4 %shard_map.82 = f32[8,2,128]{2,1,0:T(2,128)} custom-call(s32[8,128]{1,0:T(8,128)} %bitcast.4, s32[8,128]{1,0:T(8,128)} %bitcast.5, f32[8]{0:T(128)} %screen_ref.1, s32[1024,128]{1,0:T(8,128)} %cells_hbm.1, bf16[1024,128]{1,0:T(8,128)(2,1)} %mass_hbm.1, bf16[288,512]{1,0:T(8,128)(2,1)} %constant.6.clone.z_hbm, bf16[2,1536,256]{2,1,0:T(8,128)(2,1)} %constant.7.clone.y_hbm, ...), custom_call_target="tpu_custom_call" | custom-call | tf_op jit(solution)/shard_map/pallas_call | solution.py:388
  37.4 1.3 %copy.10 = f32[8,128,2]{1,2,0:T(2,128)} copy(f32[8,128,2]{1,2,0:T(2,128)} %bitcast.3) | data formatting | bytes 16384

commit v8 on v7

--- a/solution.py
+++ b/solution.py
@@ -412,7 +412,7 @@
             pltpu.VMEM((2, HELD * MEET, SPAN), f32),
             pltpu.VMEM((2, HELD, 2, KZ, KY), f32),
             pltpu.VMEM((HELD, 2, KZ, KY), f32),
-            pltpu.VMEM((DEVICES * PARTS, KY), f32),
+            pltpu.VMEM((DEVICES * PARTS + PARTS, KY), f32),
             pltpu.VMEM((DEVICES * PARTS, KY), f32),
             dma((7,)),
             dma((2,)),
@@ -421,7 +421,7 @@
             dma,
             dma,
         ]
-        + [pltpu.VMEM((Q * 8, SUB), f32)] * (UNROLL // 4),
+        + [pltpu.VMEM((Q * 8 + 8, SUB), f32)] * (UNROLL // 4),
         compiler_params=pltpu.CompilerParams(
             collective_id=0, has_side_effects=True, vmem_limit_bytes=60 << 20
         ),

time: 38.9 us -> 38.8 us (level)
  no operation moved by 1% of the time
where the time goes in v8:
time: 38.8 us; the launch traced here: 38.6 us
  Pallas kernels  37.3 us (96%)
  local copies, waits for them, and re-layouts  1.3 us (3%)
    pallas_call x1, Pallas kernels, shards(): pl.pallas_call(mesh_kernel, out_shape=jax.ShapeDtypeStruct((PL, 2, KY), f...  37.3 us
    unnamed x1, local copies, waits for them, and re-layouts  1.3 us

profile of v8, /device:TPU:1, one launch (start us, length us, event | category | flops | bytes accessed | tf_op | source)
XLA Modules:
  0.0 38.6 jit_solution(2383757024081058065)
XLA Ops:
  0.0 37.3 %shard_map.82 = f32[8,2,128]{2,1,0:T(2,128)} custom-call(s32[8,128]{1,0:T(8,128)} %bitcast.4, s32[8,128]{1,0:T(8,128)} %bitcast.5, f32[8]{0:T(128)} %screen_ref.1, s32[1024,128]{1,0:T(8,128)} %cells_hbm.1, bf16[1024,128]{1,0:T(8,128)(2,1)} %mass_hbm.1, bf16[288,512]{1,0:T(8,128)(2,1)} %constant.6.clone.z_hbm, bf16[2,1536,256]{2,1,0:T(8,128)(2,1)} %constant.7.clone.y_hbm, ...), custom_call_target="tpu_custom_call" | custom-call | tf_op jit(solution)/shard_map/pallas_call | solution.py:388
  37.3 1.3 %copy.10 = f32[8,128,2]{1,2,0:T(2,128)} copy(f32[8,128,2]{1,2,0:T(2,128)} %bitcast.3) | data formatting | bytes 16384
